TPU v7x, 256 devices: a whole 4x4x8 slice. The times are simulated.
256 devices in a mesh: seq: 4 (over x_lo, core), ctx: 64 (over x_hi, z, y).
Axes of the slice: x: 4 (x_hi: 2, x_lo: 2; x = x_hi * 2 + x_lo), y: 4, z: 8, core: 2. Of those that a mesh axis runs over, the one named last changes fastest.
Arguments:
- grad_out: bfloat16 [4, 8192, 4096], P('seq', 'ctx'), may hold values from -6 to 6
- inputs: bfloat16 [4, 8192, 4096], P('seq', 'ctx'), may hold values from -6 to 6
- residues: float32 [16, 256], replicated, may hold values from -4 to 4
- rates: float32 [16, 256], replicated, may hold values from 1.2207031e-05 to 0.0625
Outputs:
- grad_in: float32 [4, 8192, 4096], P('seq', 'ctx')
- grad_residues: float32 [16, 256], replicated
All inputs are finite; a program needn't handle non-finite values.
Results may differ from a plain program's by a relative error of at most 0.0003.
Values sent between devices are 32-bit elements; how exact they have to be, the bound alone decides.
No kernel may reach another device: no remote copies, remote signals or barrier semaphores. Data moves between devices by JAX's collectives and lax.ppermute only.
A program may use at most 128 MiB of HBM per device.

v0:
```python
import jax
import jax.numpy as jnp
from jax import lax
from jax.sharding import Mesh
from jax.sharding import PartitionSpec as P

CTX = ("ctx_0", "ctx_1", "ctx_2")


def nothing_yet(value, identity):
    return jax.tree.map(
        lambda part, zero: jnp.zeros_like(part) + jnp.asarray(zero, part.dtype), value, identity
    )


def entering(value, axes, combine, identity):
    before = start = nothing_yet(value, identity)
    running = value
    for axis in reversed(axes):
        peers, mine = (lax.axis_size(axis), lax.axis_index(axis))
        pieces = jax.tree.map(lambda part: lax.all_gather(part, axis), running)
        inside, running = (start, start)
        for k in reversed(range(peers)):
            passed = k > mine
            running = combine(running, jax.tree.map(lambda part: part[k], pieces))
            inside = jax.tree.map(lambda new, old: jnp.where(passed, new, old), running, inside)
        before = combine(inside, before)
    return before


def from_everyone(value, axis):
    peers = lax.axis_size(axis)
    return lax.all_to_all(
        jnp.broadcast_to(value[None], (peers, *value.shape)), axis, 0, 0, tiled=True
    )


def of_everyone(value, axis):
    everything = from_everyone(value, axis)
    return jnp.sum(everything, axis=0)


def local(grad_out, inputs, residues, rates):
    own_rows = grad_out.shape[1]
    model_width = grad_out.shape[2]
    mode_count = residues.shape[0]
    groups = residues.shape[1]
    per_group = model_width // groups
    shards = lax.axis_size(CTX)
    seq_count = lax.axis_size("seq")
    group_block = min(groups, 16)
    block_count = groups // group_block
    highest = lax.Precision.HIGHEST
    positions = jnp.arange(own_rows, dtype=jnp.float32)
    decays = jnp.exp(-rates[:, :, None] * positions)
    remaining = jnp.exp(-rates[:, :, None] * (own_rows - positions))
    amplitude = residues * jnp.sqrt(-jnp.expm1(-2.0 * rates) / mode_count)
    kernel = jnp.sum(amplitude[:, :, None] * decays, axis=0)
    lag_index = lax.broadcasted_iota(jnp.int32, (own_rows, own_rows), 1) - lax.broadcasted_iota(
        jnp.int32, (own_rows, own_rows), 0
    )
    causal = lag_index >= 0
    clipped = jnp.clip(lag_index, 0, own_rows - 1)
    row_of = lax.broadcasted_iota(jnp.int32, (own_rows, own_rows), 0)
    col_of = lax.broadcasted_iota(jnp.int32, (own_rows, own_rows), 1)
    diagonal_mask = row_of + col_of < own_rows
    grad_rows = grad_out[0].reshape(own_rows, groups, per_group)
    in_rows = inputs[0].reshape(own_rows, groups, per_group)

    def one_block(position):
        first_group = position * group_block
        grad_piece = lax.dynamic_slice_in_dim(grad_rows, first_group, group_block, 1)
        input_piece = lax.dynamic_slice_in_dim(in_rows, first_group, group_block, 1)
        kernel_piece = lax.dynamic_slice_in_dim(kernel, first_group, group_block, 0)
        decay_piece = lax.dynamic_slice_in_dim(decays, first_group, group_block, 1)
        tail_piece = lax.dynamic_slice_in_dim(remaining, first_group, group_block, 1)
        toeplitz = jnp.where(causal[None], jnp.take(kernel_piece, clipped, axis=1), 0.0)
        grad_wide = grad_piece.astype(jnp.float32)
        local_in = jnp.einsum("gst,tgc->sgc", toeplitz, grad_wide, precision=highest)
        summary = jnp.einsum("ngt,tgc->ngc", decay_piece, grad_wide, precision=highest)
        tail_weight = jnp.einsum(
            "ngs,sgc->ngc", tail_piece, input_piece.astype(jnp.float32), precision=highest
        )
        products = jnp.einsum(
            "sgc,tgc->gst", input_piece, grad_piece, preferred_element_type=jnp.float32
        )
        flattened = products.reshape(group_block, own_rows * own_rows)
        flattened = jnp.pad(flattened, ((0, 0), (0, own_rows)))
        skewed = flattened.reshape(group_block, own_rows, own_rows + 1)[:, :, :own_rows]
        lagged = jnp.sum(jnp.where(diagonal_mask[None], skewed, 0.0), axis=1)
        local_grad = jnp.sum(decay_piece * lagged[None], axis=2)
        return (local_in, summary, tail_weight, local_grad)

    local_in, summary, tail_weight, local_grad = lax.map(
        one_block, jnp.arange(block_count, dtype=jnp.int32)
    )
    local_in = jnp.moveaxis(local_in, 0, 1).reshape(own_rows, groups, per_group)
    summary = jnp.moveaxis(summary, 0, 1).reshape(mode_count, model_width)
    tail_weight = jnp.moveaxis(tail_weight, 0, 1).reshape(mode_count, groups, per_group)
    local_grad = jnp.moveaxis(local_grad, 0, 1).reshape(mode_count, groups)
    decay_shard = jnp.exp(-rates * own_rows)

    def compose(earlier, latter):
        joined = latter[0].reshape(mode_count, groups, per_group) + latter[1][:, :, None] * earlier[
            0
        ].reshape(mode_count, groups, per_group)
        return (joined.reshape(mode_count, model_width), latter[1] * earlier[1])

    identity = (
        jnp.zeros((mode_count, model_width), jnp.float32),
        jnp.ones((mode_count, groups), jnp.float32),
    )
    scanned = entering((summary, decay_shard), CTX, compose, identity)
    incoming = scanned[0].reshape(mode_count, groups, per_group)
    carry_in = jnp.einsum(
        "ngs,ngc->sgc", amplitude[:, :, None] * remaining, incoming, precision=highest
    )
    grad_in = (local_in + carry_in).reshape(1, own_rows, model_width)
    partial_value = local_grad + jnp.sum(tail_weight * incoming, axis=2)
    along = of_everyone(partial_value, CTX)
    total = of_everyone(along, "seq")
    factor = jnp.sqrt(-jnp.expm1(-2.0 * rates) / float(seq_count * shards * own_rows * per_group))
    return (grad_in, total * factor)


def solution(mesh):
    torus = Mesh(
        mesh.devices.reshape(mesh.shape["seq"], 2, 8, 4), ("seq", "ctx_0", "ctx_1", "ctx_2")
    )
    return jax.shard_map(
        local,
        mesh=torus,
        in_specs=(P("seq", CTX, None), P("seq", CTX, None), P(), P()),
        out_specs=(P("seq", CTX, None), P()),
        check_vma=False,
    )
```

profile of v0, /device:TPU:1, one launch (start us, length us, event | category | flops | bytes accessed | tf_op | source)
XLA Modules:
  0.0 1438.3 jit_solution(1741051747657415870)
XLA Ops:
  14.6 1174.7 %while.21 = (s32[]{:T(128)}, f32[16,128,16,16]{1,3,2,0:T(8,128)}, f32[16,16,16,16]{1,3,2,0:T(8,128)}, f32[16,16,16,16]{1,3,2,0:T(8,128)}, f32[16,16,16]{1,2,0:T(...) while((s32[]{:T(128)}, f32[16,128,16,16]{1,3,2,0:T(8,128)}, ...), condition=%wide.region_4.5_spmd.clone.clone.clone, body=%wide.region_1.4_spmd.clone.clone.sunk.clone | while | flops 72693504 | bytes 15063247 | solution.py:94
  16.0 54.5 %gather_fusion = f32[16384,16]{1,0:T(8,128)} fusion(f32[16,128]{0,1:T(8,128)S(1)} %copy.296, s32[16384]{0:T(1024)S(1)} %fusion.102), kind=kCustom, calls=%fused_computation.clone.clone.1.clone | custom fusion | bytes 2162688 | tf_op jit(solution)/shard_map/while/body/eval_jaxpr/jit(_take)/gather | solution.py:77
  89.4 54.5 %gather_fusion = f32[16384,16]{1,0:T(8,128)} fusion(f32[16,128]{0,1:T(8,128)S(1)} %copy.296, s32[16384]{0:T(1024)S(1)} %fusion.102), kind=kCustom, calls=%fused_computation.clone.clone.1.clone | custom fusion | bytes 2162688 | tf_op jit(solution)/shard_map/while/body/eval_jaxpr/jit(_take)/gather | solution.py:77
  162.8 54.5 %gather_fusion = f32[16384,16]{1,0:T(8,128)} fusion(f32[16,128]{0,1:T(8,128)S(1)} %copy.296, s32[16384]{0:T(1024)S(1)} %fusion.102), kind=kCustom, calls=%fused_computation.clone.clone.1.clone | custom fusion | bytes 2162688 | tf_op jit(solution)/shard_map/while/body/eval_jaxpr/jit(_take)/gather | solution.py:77
  236.2 54.5 %gather_fusion = f32[16384,16]{1,0:T(8,128)} fusion(f32[16,128]{0,1:T(8,128)S(1)} %copy.296, s32[16384]{0:T(1024)S(1)} %fusion.102), kind=kCustom, calls=%fused_computation.clone.clone.1.clone | custom fusion | bytes 2162688 | tf_op jit(solution)/shard_map/while/body/eval_jaxpr/jit(_take)/gather | solution.py:77
  309.6 54.5 %gather_fusion = f32[16384,16]{1,0:T(8,128)} fusion(f32[16,128]{0,1:T(8,128)S(1)} %copy.296, s32[16384]{0:T(1024)S(1)} %fusion.102), kind=kCustom, calls=%fused_computation.clone.clone.1.clone | custom fusion | bytes 2162688 | tf_op jit(solution)/shard_map/while/body/eval_jaxpr/jit(_take)/gather | solution.py:77
  383.1 54.5 %gather_fusion = f32[16384,16]{1,0:T(8,128)} fusion(f32[16,128]{0,1:T(8,128)S(1)} %copy.296, s32[16384]{0:T(1024)S(1)} %fusion.102), kind=kCustom, calls=%fused_computation.clone.clone.1.clone | custom fusion | bytes 2162688 | tf_op jit(solution)/shard_map/while/body/eval_jaxpr/jit(_take)/gather | solution.py:77
  456.5 54.5 %gather_fusion = f32[16384,16]{1,0:T(8,128)} fusion(f32[16,128]{0,1:T(8,128)S(1)} %copy.296, s32[16384]{0:T(1024)S(1)} %fusion.102), kind=kCustom, calls=%fused_computation.clone.clone.1.clone | custom fusion | bytes 2162688 | tf_op jit(solution)/shard_map/while/body/eval_jaxpr/jit(_take)/gather | solution.py:77
  529.9 54.5 %gather_fusion = f32[16384,16]{1,0:T(8,128)} fusion(f32[16,128]{0,1:T(8,128)S(1)} %copy.296, s32[16384]{0:T(1024)S(1)} %fusion.102), kind=kCustom, calls=%fused_computation.clone.clone.1.clone | custom fusion | bytes 2162688 | tf_op jit(solution)/shard_map/while/body/eval_jaxpr/jit(_take)/gather | solution.py:77
  603.3 54.5 %gather_fusion = f32[16384,16]{1,0:T(8,128)} fusion(f32[16,128]{0,1:T(8,128)S(1)} %copy.296, s32[16384]{0:T(1024)S(1)} %fusion.102), kind=kCustom, calls=%fused_computation.clone.clone.1.clone | custom fusion | bytes 2162688 | tf_op jit(solution)/shard_map/while/body/eval_jaxpr/jit(_take)/gather | solution.py:77
  676.7 54.5 %gather_fusion = f32[16384,16]{1,0:T(8,128)} fusion(f32[16,128]{0,1:T(8,128)S(1)} %copy.296, s32[16384]{0:T(1024)S(1)} %fusion.102), kind=kCustom, calls=%fused_computation.clone.clone.1.clone | custom fusion | bytes 2162688 | tf_op jit(solution)/shard_map/while/body/eval_jaxpr/jit(_take)/gather | solution.py:77
  750.2 54.5 %gather_fusion = f32[16384,16]{1,0:T(8,128)} fusion(f32[16,128]{0,1:T(8,128)S(1)} %copy.296, s32[16384]{0:T(1024)S(1)} %fusion.102), kind=kCustom, calls=%fused_computation.clone.clone.1.clone | custom fusion | bytes 2162688 | tf_op jit(solution)/shard_map/while/body/eval_jaxpr/jit(_take)/gather | solution.py:77
  823.6 54.5 %gather_fusion = f32[16384,16]{1,0:T(8,128)} fusion(f32[16,128]{0,1:T(8,128)S(1)} %copy.296, s32[16384]{0:T(1024)S(1)} %fusion.102), kind=kCustom, calls=%fused_computation.clone.clone.1.clone | custom fusion | bytes 2162688 | tf_op jit(solution)/shard_map/while/body/eval_jaxpr/jit(_take)/gather | solution.py:77
  897.0 54.5 %gather_fusion = f32[16384,16]{1,0:T(8,128)} fusion(f32[16,128]{0,1:T(8,128)S(1)} %copy.296, s32[16384]{0:T(1024)S(1)} %fusion.102), kind=kCustom, calls=%fused_computation.clone.clone.1.clone | custom fusion | bytes 2162688 | tf_op jit(solution)/shard_map/while/body/eval_jaxpr/jit(_take)/gather | solution.py:77
  970.4 54.5 %gather_fusion = f32[16384,16]{1,0:T(8,128)} fusion(f32[16,128]{0,1:T(8,128)S(1)} %copy.296, s32[16384]{0:T(1024)S(1)} %fusion.102), kind=kCustom, calls=%fused_computation.clone.clone.1.clone | custom fusion | bytes 2162688 | tf_op jit(solution)/shard_map/while/body/eval_jaxpr/jit(_take)/gather | solution.py:77
  1043.9 54.5 %gather_fusion = f32[16384,16]{1,0:T(8,128)} fusion(f32[16,128]{0,1:T(8,128)S(1)} %copy.296, s32[16384]{0:T(1024)S(1)} %fusion.102), kind=kCustom, calls=%fused_computation.clone.clone.1.clone | custom fusion | bytes 2162688 | tf_op jit(solution)/shard_map/while/body/eval_jaxpr/jit(_take)/gather | solution.py:77
  1117.3 54.5 %gather_fusion = f32[16384,16]{1,0:T(8,128)} fusion(f32[16,128]{0,1:T(8,128)S(1)} %copy.296, s32[16384]{0:T(1024)S(1)} %fusion.102), kind=kCustom, calls=%fused_computation.clone.clone.1.clone | custom fusion | bytes 2162688 | tf_op jit(solution)/shard_map/while/body/eval_jaxpr/jit(_take)/gather | solution.py:77
  1192.3 10.5 all-gather
  1224.1 20.7 %all_gather.27 = f32[8,16,256]{2,1,0:T(8,128)S(1)} all-gather(f32[1,16,256]{2,1,0:T(8,128)S(1)} %copy-done.56), channel_id=1, replica_groups=mesh['seq'=4,'ctx_0'=2,'ctx_1'=8,'ctx_2'=4] {'ctx_1'}, dimensions={0}, use_global_device_ids=true | all-gather | bytes 147456 | tf_op jit(solution)/shard_map/all_gather | solution.py:21
  1338.0 11.1 fusion.38
  1350.3 10.8 all-to-all-start
  1391.0 13.0 multiply_add_fusion
  1404.7 14.2 all-to-all-start.1
  1419.0 8.8 bitcast_add_fusion
  (516 shorter events, 451.2 us)
Async XLA Ops:
  7.2 1213.6 %all-gather.4.cloned.1.call-start = ((), (), s32[]{:S(2)}) async-start(), calls=%async_computation.2 | async-start | bytes 1310720 | tf_op jit(solution)/shard_map/all_gather | solution.py:21
  9.8 4.8 copy-start.24
  1192.2 111.2 %all-gather.6.cloned.1.call-start = ((), (), s32[]{:S(2)}) async-start(), calls=%async_computation.3 | async-start | bytes 2359296 | tf_op jit(solution)/shard_map/all_gather | solution.py:21
  1203.4 7.9 copy-start.44
  1203.4 19.7 %copy-start.42 = (f32[16,256]{1,0:T(8,128)}, f32[16,256]{1,0:T(8,128)S(1)}, u32[]{:S(2)}) copy-start(f32[16,256]{1,0:T(8,128)S(1)} %get-tuple-element.376) | copy-start | bytes 49156
  1203.4 19.8 %copy-start.40 = (f32[16,256]{1,0:T(8,128)}, f32[16,256]{1,0:T(8,128)S(1)}, u32[]{:S(2)}) copy-start(f32[16,256]{1,0:T(8,128)S(1)} %get-tuple-element.375) | copy-start | bytes 49156
  1214.2 9.8 copy-start.56
  1223.1 73.9 %copy-start.21 = (f32[1,16,4096]{2,1,0:T(8,128)}, f32[1,16,4096]{2,1,0:T(8,128)S(1)}, u32[]{:S(2)}) copy-start(f32[1,16,4096]{2,1,0:T(8,128)S(1)} %get-tuple-element.349) | copy-start | bytes 786436
  1223.1 74.5 %copy-start.19 = (f32[1,16,4096]{2,1,0:T(8,128)}, f32[1,16,4096]{2,1,0:T(8,128)S(1)}, u32[]{:S(2)}) copy-start(f32[1,16,4096]{2,1,0:T(8,128)S(1)} %get-tuple-element.348) | copy-start | bytes 786436
  1223.1 76.4 %copy-start.17 = (f32[1,16,4096]{2,1,0:T(8,128)}, f32[1,16,4096]{2,1,0:T(8,128)S(1)}, u32[]{:S(2)}) copy-start(f32[1,16,4096]{2,1,0:T(8,128)S(1)} %get-tuple-element.347) | copy-start | bytes 786436
  1223.1 78.4 %copy-start.15 = (f32[1,16,4096]{2,1,0:T(8,128)}, f32[1,16,4096]{2,1,0:T(8,128)S(1)}, u32[]{:S(2)}) copy-start(f32[1,16,4096]{2,1,0:T(8,128)S(1)} %get-tuple-element.345) | copy-start | bytes 786436
  1279.2 12.2 copy-start.23
  1305.7 26.3 %copy-start.2 = (f32[1,16,4096]{2,1,0:T(8,128)}, f32[1,16,4096]{2,1,0:T(8,128)S(1)}, u32[]{:S(2)}) copy-start(f32[1,16,4096]{2,1,0:T(8,128)S(1)} %get-tuple-element.339) | copy-start | bytes 786436
  1305.7 28.3 %copy-start = (f32[1,16,4096]{2,1,0:T(8,128)}, f32[1,16,4096]{2,1,0:T(8,128)S(1)}, u32[]{:S(2)}) copy-start(f32[1,16,4096]{2,1,0:T(8,128)S(1)} %get-tuple-element.338) | copy-start | bytes 786436
  1319.3 8.8 copy-start.6
  1319.3 10.7 copy-start.4
  1338.0 11.1 copy-start.53
  1349.1 12.1 copy-start.32
  1349.1 12.7 copy-start.22
  1350.3 13.6 copy-start.20
  1350.3 53.7 %all-to-all-start = ((f32[64,16,256]{2,1,0:T(8,128)}), f32[64,16,256]{2,1,0:T(8,128)S(1)}, u32[]{:S(2)}, u32[]{:S(2)}) async-start(f32[64,16,256]{2,1,0:T(8,128)} %broadcast_in_dim.112), calls=%async_computation | async-start | bytes 2097152 | tf_op jit(solution)/shard_map/all_to_all | solution.py:33
  1391.0 27.9 %copy-start.25 = (f32[16,256]{0,1:T(8,128)S(1)}, f32[16,256]{0,1:T(8,128)}, u32[]{:S(2)}) copy-start(f32[16,256]{0,1:T(8,128)} %copy-done.24) | copy-start | bytes 49156
  1391.0 27.9 %copy-start.27 = (f32[16,256]{0,1:T(8,128)S(1)}, f32[16,256]{0,1:T(8,128)}, u32[]{:S(2)}) copy-start(f32[16,256]{0,1:T(8,128)} %copy-done.26) | copy-start | bytes 49156
  1404.7 25.9 %all-to-all-start.1 = ((f32[4,16,256]{2,1,0:T(8,128)}), f32[4,16,256]{2,1,0:T(8,128)S(1)}, u32[]{:S(2)}, u32[]{:S(2)}) async-start(f32[4,16,256]{2,1,0:T(8,128)} %broadcast_in_dim.113), calls=%async_computation.1 | async-start | bytes 131072 | tf_op jit(solution)/shard_map/all_to_all | solution.py:33
  (39 other events, 138.2 us)
Sparse Core Ops, SparseCore 0:
  1192.4 28.3 all-gather.3
  1223.2 39.7 all-gather.5
where the time goes:
time: 1450 us; the launch traced here: 1440 us
  local copies, waits for them, and re-layouts  1160 us (80%)
  matrix products  126 us (9%)
  other arithmetic  54.7 us (4%)
  blocking collectives  43.6 us (3%)
  starting transfers between devices  25.1 us (2%)
  between operations  15 us (1%)
    gather x32, local copies, waits for them, and re-layouts, one_block(): jnp.take(kernel_piece, clipped, axis=1)  955 us
    another operation x28, local copies, waits for them, and re-layouts, compose(): latter[0].reshape(mode_count, groups, per_group)  58.1 us
    mul x52, local copies, waits for them, and re-layouts, compose(): latter[1][:, :, None] * earlier[0].reshape(mode_count, groups, per_group)  54.5 us
    all_gather x4, blocking collectives, entering(): pieces = jax.tree.map(lambda part: lax.all_gather(part, axis), running)  43.6 us
    reshape x16, local copies, waits for them, and re-layouts, one_block(): flattened.reshape(group_block, own_rows, own_rows + 1)[:, :, :own_rows]  39.7 us
    dot_general x16, matrix products, one_block(): jnp.einsum('gst,tgc->sgc', toeplitz, grad_wide, precision=highest)  39.4 us
    dot_general x16, matrix products, one_block(): jnp.einsum('ngs,sgc->ngc', tail_piece, input_piece.astype(jnp.float32), p...  29.2 us
    dot_general x16, matrix products, one_block(): jnp.einsum('ngt,tgc->ngc', decay_piece, grad_wide, precision=highest)  29.2 us
  transfers between devices with their start and end apart: 4, of which 1 were waited for; matrix products, arithmetic and copies ran while one was open for 8% of the time, Pallas kernels for 0%

commit v1 on v0

v1 whole, which is shorter than its diff:
```python
import functools

import jax
import jax.numpy as jnp
from jax import lax
from jax.experimental import pallas as pl
from jax.experimental.pallas import tpu as pltpu
from jax.sharding import Mesh
from jax.sharding import PartitionSpec as P

CTX = ("ctx_0", "ctx_1", "ctx_2")
LANES = 128
CG = 16
GT = LANES // CG
SUB = 32
F32 = jnp.float32
BF16 = jnp.bfloat16
HIGHEST = lax.Precision.HIGHEST


def iota(shape, dim):
    return lax.broadcasted_iota(jnp.int32, shape, dim)


def split(value):
    high = value.astype(BF16)
    return high, (value - high.astype(F32)).astype(BF16)


def dot(a, b, dims=((1,), (0,))):
    return lax.dot_general(a, b, (dims, ((), ())), preferred_element_type=F32)


def group_columns(table, first):
    groups = table.shape[1]
    turned = pltpu.roll(table, (groups - first) % groups, 1)
    return [jnp.broadcast_to(turned[:, g : g + 1], (table.shape[0], LANES)) for g in range(GT)]


def own_group(full, rows):
    group_of = iota((rows, LANES), 1) // CG
    kept = full[:rows]
    for g in range(1, GT):
        kept = jnp.where(group_of == g, full[g * rows : (g + 1) * rows], kept)
    return kept


def summary_kernel(rates_ref, grad_ref, in_ref, out_ref):
    rows = grad_ref.shape[0]
    modes = rates_ref.shape[0]
    half = modes // 2
    tiles = grad_ref.shape[1] // LANES
    all_tiles = out_ref.shape[0] // (2 * 17)
    pos = iota((modes, LANES), 1).astype(F32)
    lane_group = iota((GT, LANES), 1) // CG
    own = lane_group == iota((GT, LANES), 0)
    lane = iota((GT, LANES), 1)
    cell = iota((half, LANES), 1)
    cell_row = iota((half, LANES), 0)

    def one_tile(k, carry):
        tile = pl.program_id(0) * tiles + k
        at = pl.ds(pl.multiple_of(k * LANES, LANES), LANES)
        grad = grad_ref[:, at]
        inp = in_ref[:, at]
        columns = group_columns(rates_ref[...], tile * GT)
        decays = [jnp.exp(-r * pos) for r in columns]
        decay = jnp.concatenate(decays, 0)
        tails = jnp.concatenate([jnp.exp(-r * (rows - pos)) for r in columns], 0)
        left = jnp.concatenate(split(decay), 1)
        summary = own_group(dot(left, jnp.concatenate([grad, grad], 0)), modes)
        left = jnp.concatenate(split(tails), 1)
        tail = own_group(dot(left, jnp.concatenate([inp, inp], 0)), modes)

        wide = inp.astype(F32)
        lefts = []
        rights = []
        for i in range(rows // SUB):
            piece = wide[i * SUB : (i + 1) * SUB]
            spread = jnp.broadcast_to(piece[:, None, :], (SUB, GT, LANES))
            spread = jnp.where(own[None], spread, 0.0)
            lefts.append(spread.reshape(SUB * GT, LANES).astype(BF16))
            window = grad[i * SUB :]
            if i:
                window = jnp.concatenate([window, jnp.zeros((i * SUB, LANES), BF16)], 0)
            rights.append(window)
        pairs = dot(jnp.concatenate(lefts, 1), jnp.concatenate(rights, 1), ((1,), (1,)))
        lagged = pairs[:GT]
        for j in range(1, SUB):
            part = jnp.where(lane >= j, pairs[j * GT : (j + 1) * GT], 0.0)
            lagged = lagged + pltpu.roll(part, LANES - j, 1)
        sums = [jnp.zeros((half, LANES), F32) for _ in range(2)]
        for g in range(GT):
            weighted = decays[g] * lagged[g : g + 1]
            total = jnp.sum(weighted, axis=1, keepdims=True)
            place = cell == cell_row + g * CG
            for a in range(2):
                sums[a] = jnp.where(place, total[a * half : (a + 1) * half], sums[a])
        for a in range(2):
            base = (a * all_tiles + tile) * 17
            out_ref[pl.ds(base, 8), :] = summary[a * half : (a + 1) * half]
            out_ref[pl.ds(base + 8, 8), :] = tail[a * half : (a + 1) * half]
            out_ref[pl.ds(base + 16, 1), :] = jnp.sum(sums[a], axis=0, keepdims=True)
        return carry

    lax.fori_loop(0, tiles, one_tile, 0, unroll=2)


def local_kernel(rates_ref, amp_ref, rate_row_ref, amp_row_ref, grad_ref, out_ref, high_ref, low_ref):
    rows = grad_ref.shape[0]
    modes = rates_ref.shape[0]
    tiles = grad_ref.shape[1] // LANES
    pos = iota((modes, LANES), 1).astype(F32)
    ahead = iota((SUB, LANES), 1) >= iota((SUB, LANES), 0)
    to_end = (rows - iota((rows, LANES), 0)).astype(F32)

    def one_tile(k, carry):
        tile = pl.program_id(0) * tiles + k
        at = pl.ds(pl.multiple_of(k * LANES, LANES), LANES)
        grad = grad_ref[:, at]
        columns = group_columns(rates_ref[...], tile * GT)
        amps = group_columns(amp_ref[...], tile * GT)
        highs = []
        lows = []
        for r, a in zip(columns, amps):
            kernel = jnp.sum(a * jnp.exp(-r * pos), axis=0, keepdims=True)
            high = kernel.astype(BF16).astype(F32)
            for part, into in ((high, highs), (kernel - high, lows)):
                turned = pltpu.roll(
                    jnp.broadcast_to(part, (SUB, LANES)), 0, 1, stride=1, stride_axis=0
                )
                into.append(jnp.where(ahead, turned, 0.0).astype(BF16))
        left = jnp.concatenate([jnp.concatenate(highs, 0), jnp.concatenate(lows, 0)], 1)
        for i in range(rows // SUB):
            window = grad[i * SUB :]
            if i:
                window = jnp.concatenate([window, jnp.zeros((i * SUB, LANES), BF16)], 0)
            full = dot(left, jnp.concatenate([window, window], 0))
            out_ref[i * SUB : (i + 1) * SUB, at] = own_group(full, SUB)
        weight = amp_row_ref[:, at] * jnp.exp(-rate_row_ref[:, at] * to_end)
        high, low = split(weight)
        high_ref[:, at] = high
        low_ref[:, at] = low
        return carry

    lax.fori_loop(0, tiles, one_tile, 0, unroll=2)


def scan_kernel(decay_ref, in_ref, out_ref):
    shards = in_ref.shape[0] // 17
    decay = decay_ref[...]
    state = jnp.zeros((8, LANES), F32)
    total = jnp.zeros((8, LANES), F32)
    row = jnp.zeros((1, LANES), F32)
    for j in reversed(range(shards)):
        out_ref[9 * j : 9 * j + 8, :] = state
        total = total + in_ref[17 * j + 8 : 17 * j + 16, :] * state
        row = row + in_ref[17 * j + 16 : 17 * j + 17, :]
        state = in_ref[17 * j : 17 * j + 8, :] + decay * state
    same = iota((LANES, LANES), 0) // CG == iota((LANES, LANES), 1) // CG
    summed = lax.dot_general(
        total,
        same.astype(F32),
        (((1,), (0,)), ((), ())),
        precision=HIGHEST,
        preferred_element_type=F32,
    )
    place = iota((8, LANES), 1) % CG == iota((8, LANES), 0)
    row = row + jnp.sum(jnp.where(place, summed, 0.0), axis=0, keepdims=True)
    for j in range(shards):
        out_ref[9 * j + 8 : 9 * j + 9, :] = row


def carry_kernel(state_ref, local_ref, high_ref, low_ref, out_ref):
    tiles = out_ref.shape[1] // LANES
    all_tiles = state_ref.shape[0] // (2 * 9)
    lane_group = iota((2 * 8, LANES), 1) // CG

    def one_tile(k, carry):
        tile = pl.program_id(0) * tiles + k
        at = pl.ds(pl.multiple_of(k * LANES, LANES), LANES)
        state = jnp.concatenate(
            [state_ref[pl.ds((a * all_tiles + tile) * 9, 8), :] for a in range(2)], 0
        )
        rights = []
        for part in split(state):
            part = part.astype(F32)
            rights.append(
                jnp.concatenate(
                    [jnp.where(lane_group == g, part, 0.0).astype(BF16) for g in range(GT)], 0
                )
            )
        high = high_ref[:, at]
        left = jnp.concatenate([high, low_ref[:, at], high], 1)
        right = jnp.concatenate([rights[0], rights[0], rights[1]], 0)
        out_ref[:, at] = local_ref[:, at] + dot(left, right)
        return carry

    lax.fori_loop(0, tiles, one_tile, 0, unroll=2)


def finish_kernel(factor_ref, a_ref, b_ref, c_ref, d_ref, out_ref):
    total = (a_ref[...] + b_ref[...]) + (c_ref[...] + d_ref[...])
    count = total.shape[0] // 2
    groups = out_ref.shape[1]
    pick = (iota((count, groups), 0) == iota((count, groups), 1) // GT).astype(F32)
    keep = iota((GT, CG, groups), 0) == iota((GT, CG, groups), 2) % GT
    for a in range(2):
        spread = lax.dot_general(
            total[a * count : (a + 1) * count],
            pick,
            (((0,), (0,)), ((), ())),
            precision=HIGHEST,
            preferred_element_type=F32,
        ).reshape(GT, CG, groups)
        cells = jnp.sum(jnp.where(keep, spread, 0.0), axis=0)
        out_ref[a * 8 : (a + 1) * 8, :] = cells[:8] * factor_ref[a * 8 : (a + 1) * 8, :]


def whole(shape):
    return pl.BlockSpec(shape, lambda *_: (0,) * len(shape))


def local(grad_out, inputs, residues, rates):
    _, rows, width = grad_out.shape
    modes, groups = residues.shape
    tiles = width // LANES
    shards = lax.axis_size(CTX)
    seqs = lax.axis_size("seq_x") * lax.axis_size("seq_core")
    steps = 4
    block = width // steps
    slab = pl.BlockSpec((rows, block), lambda q: (0, q))
    grad = grad_out[0]
    inp = inputs[0]
    vmem = pltpu.CompilerParams(vmem_limit_bytes=48 * 1024 * 1024)

    sent = pl.pallas_call(
        summary_kernel,
        grid=(steps,),
        in_specs=[whole((modes, groups)), slab, slab],
        out_specs=whole((shards * 17, LANES)),
        out_shape=jax.ShapeDtypeStruct((shards * 17, LANES), F32),
        compiler_params=vmem,
        name="summary",
    )(rates, grad, inp)
    got = lax.all_to_all(sent.reshape(shards, 1, 17 * LANES), CTX, 0, 0, tiled=True)

    amplitude = residues * jnp.sqrt(-jnp.expm1(-2.0 * rates) / modes)
    factor = jnp.sqrt(-jnp.expm1(-2.0 * rates) / float(seqs * shards * rows * (width // groups)))
    place = lax.axis_index(CTX)
    half = modes // 2
    own_rates = lax.dynamic_slice(
        rates, (place // tiles * half, place % tiles * GT), (half, GT)
    )
    decay = jnp.repeat(jnp.exp(-own_rates * rows), CG, axis=1)

    row = pl.BlockSpec((1, block), lambda q: (0, q))
    local_in, high, low = pl.pallas_call(
        local_kernel,
        grid=(steps,),
        in_specs=[whole((modes, groups)), whole((modes, groups)), row, row, slab],
        out_specs=[slab, slab, slab],
        out_shape=[
            jax.ShapeDtypeStruct((rows, width), F32),
            jax.ShapeDtypeStruct((rows, width), BF16),
            jax.ShapeDtypeStruct((rows, width), BF16),
        ],
        compiler_params=vmem,
        name="local",
        cost_estimate=pl.CostEstimate(
            flops=8 * 10**9, bytes_accessed=5 * 2**20, transcendentals=10**6
        ),
    )(rates, amplitude, rates.T.reshape(1, width), amplitude.T.reshape(1, width), grad)

    states = pl.pallas_call(
        scan_kernel,
        out_shape=jax.ShapeDtypeStruct((shards * 9, LANES), F32),
        name="scan",
    )(decay, got.reshape(shards * 17, LANES))
    back = lax.all_to_all(states.reshape(shards, 1, 9 * LANES), CTX, 0, 0, tiled=True)

    mine = back[:, 0, 8 * LANES :]
    others = [mine]
    for bits in (1, 2, 3):
        pairs = [(d, d ^ bits) for d in range(4)]
        others.append(lax.ppermute(mine, ("seq_x", "seq_core"), pairs))
    grad_in = pl.pallas_call(
        carry_kernel,
        grid=(steps,),
        in_specs=[whole((shards * 9, LANES)), slab, slab, slab],
        out_specs=slab,
        out_shape=jax.ShapeDtypeStruct((rows, width), F32),
        compiler_params=vmem,
        name="carry",
        cost_estimate=pl.CostEstimate(
            flops=8 * 10**8, bytes_accessed=7 * 2**20, transcendentals=0
        ),
    )(back.reshape(shards * 9, LANES), local_in, high, low)
    grad_res = pl.pallas_call(
        finish_kernel,
        out_shape=jax.ShapeDtypeStruct((modes, groups), F32),
        name="finish",
    )(factor, *others)
    return grad_in[None], grad_res


def solution(mesh):
    torus = Mesh(
        mesh.devices.reshape(2, 2, 2, 8, 4), ("seq_x", "seq_core", "ctx_0", "ctx_1", "ctx_2")
    )
    seq = ("seq_x", "seq_core")
    return jax.shard_map(
        local,
        mesh=torus,
        in_specs=(P(seq, CTX, None), P(seq, CTX, None), P(), P()),
        out_specs=(P(seq, CTX, None), P()),
        check_vma=False,
    )
```

time: 1450 us -> 87 us (0.06)
  local copies, waits for them, and re-layouts: 1160 us -> 9.19 us
  matrix products: 126 us -> 0 us
  other arithmetic: 54.7 us -> 0.71 us
  blocking collectives: 43.6 us -> 0 us
  Pallas kernels: 0 us -> 34.4 us
    gather x32 -> x0, local copies, waits for them, and re-layouts: 955 us -> none  [one_block(): jnp.take(kernel_piece, clipped, axis=1)]
    dot_general x65 -> x0, matrix products: 126 us -> none  [the longest x16 39.4 us: one_block(): jnp.einsum('gst,tgc->sgc', toeplitz, grad_wide, precision=highest)]
    another operation x29 -> x0, local copies, waits for them, and re-layouts: 61 us -> none  [the longest x28 58.1 us: compose(): latter[0].reshape(mode_count, groups, per_group)]
    mul x54 -> x0, local copies, waits for them, and re-layouts: 55.4 us -> none  [the longest x52 54.5 us: compose(): latter[1][:, :, None] * earlier[0].reshape(mode_count, groups, per_group)]
    all_gather x4 -> x0, blocking collectives: 43.6 us -> none  [entering(): pieces = jax.tree.map(lambda part: lax.all_gather(part, axis), running)]
    reshape x16 -> x3, local copies, waits for them, and re-layouts: 39.7 us -> 0.9 us  [the longest x1 0.68 us: local(): decay = jnp.repeat(jnp.exp(-own_rates * rows), CG, axis=1)]
    pallas_call x0 -> x5, Pallas kernels: none -> 34.4 us  [the longest x1 14.1 us: local(): pl.pallas_call(local_kernel, grid=(steps,), in_specs=[whole((modes, group...]
    reduce_sum x35 -> x0, other arithmetic: 28.9 us -> none  [the longest x16 16.2 us: one_block(): local_grad = jnp.sum(decay_piece * lagged[None], axis=2)]
  transfers between devices with their start and end apart: 4 -> 5, of which waited for: 1 -> 1; matrix products, arithmetic and copies ran while one was open for 8% -> 2% of each run, Pallas kernels for 0% -> 22%
where the time goes in v1:
time: 87 us; the launch traced here: 86.4 us
  Pallas kernels  34.4 us (40%)
  starting transfers between devices  25.1 us (29%)
  waiting for transfers between devices  16.3 us (19%)
  local copies, waits for them, and re-layouts  9.19 us (11%)
    all_to_all x1, waiting for transfers between devices, local(): lax.all_to_all(sent.reshape(shards, 1, 17 * LANES), CTX, 0, 0, tiled=True)  16.3 us
    all_to_all x1, starting transfers between devices, local(): lax.all_to_all(sent.reshape(shards, 1, 17 * LANES), CTX, 0, 0, tiled=True)  15.1 us
    pallas_call x1, Pallas kernels, local(): pl.pallas_call(local_kernel, grid=(steps,), in_specs=[whole((modes, group...  14.1 us
    pallas_call x1, Pallas kernels, local(): pl.pallas_call(summary_kernel, grid=(steps,), in_specs=[whole((modes, gro...  11.8 us
    unnamed x26, local copies, waits for them, and re-layouts  7.98 us
    all_to_all x1, starting transfers between devices, local(): lax.all_to_all(states.reshape(shards, 1, 9 * LANES), CTX, 0, 0, tiled=True)  6.94 us
    pallas_call x1, Pallas kernels, local(): pl.pallas_call(carry_kernel, grid=(steps,), in_specs=[whole((shards * 9,...  4.5 us
    ppermute x3, starting transfers between devices, local(): others.append(lax.ppermute(mine, ('seq_x', 'seq_core'), pairs))  3.02 us
  transfers between devices with their start and end apart: 5, of which 1 were waited for; matrix products, arithmetic and copies ran while one was open for 2% of the time, Pallas kernels for 22%

profile of v1, /device:TPU:1, one launch (start us, length us, event | category | flops | bytes accessed | tf_op | source)
XLA Modules:
  0.0 86.4 jit_solution(15590761709627680589)
XLA Ops:
  0.6 1.2 %copy-done.2 = bf16[1,128,4096]{2,1,0:T(8,128)(2,1)S(1)} copy-done((bf16[1,128,4096]{2,1,0:T(8,128)(2,1)S(1)}, bf16[1,128,4096]{2,1,0:T(8,128)(2,1)}, u32[]{:S(2)}) %copy-start.2) | copy-done | bytes 1048600
  1.9 1.2 %copy-done.3 = bf16[1,128,4096]{2,1,0:T(8,128)(2,1)S(1)} copy-done((bf16[1,128,4096]{2,1,0:T(8,128)(2,1)S(1)}, bf16[1,128,4096]{2,1,0:T(8,128)(2,1)}, u32[]{:S(2)}) %copy-start.3) | copy-done | bytes 1048600
  3.1 0.7 copy-done.5
  3.8 11.8 %summary.1 = f32[1088,128]{1,0:T(8,128)} custom-call(f32[16,256]{1,0:T(8,128)S(1)} %copy-done.5, bf16[128,4096]{1,0:T(8,128)(2,1)S(1)} %bitcast.14, bf16[128,4096]{1,0:T(8,128)(2,1)S(1)} %bitcast.13), custom_call_target="tpu_custom_call" | custom-call | tf_op jit(solution)/shard_map/summary/pallas_call | solution.py:237
  15.6 15.1 %all-to-all-start = ((f32[64,1,2176]{2,1,0:T(1,128)}), f32[64,1,2176]{2,1,0:T(1,128)S(1)}, u32[]{:S(2)}, u32[]{:S(2)}) async-start(f32[64,1,2176]{2,1,0:T(1,128)} %bitcast.2), calls=%async_computation | async-start | bytes 1114112 | tf_op jit(solution)/shard_map/all_to_all | solution.py:246
  30.9 0.7 reshape.25.decay_ref
  31.6 0.6 multiply_sqrt_fusion
  32.2 0.1 copy.12
  32.3 0.1 reshape.31.amp_row_ref
  32.4 0.1 copy.11
  32.5 0.1 reshape.30.rate_row_ref
  32.7 16.3 %all-to-all-done = f32[64,1,2176]{2,1,0:T(1,128)S(1)} async-done(((f32[64,1,2176]{2,1,0:T(1,128)}), f32[64,1,2176]{2,1,0:T(1,128)S(1)}, u32[]{:S(2)}, u32[]{:S(2)}) %all-to-all-start) | async-done | bytes 557088 | tf_op jit(solution)/shard_map/all_to_all | solution.py:246
  48.9 0.8 copy-done.7
  49.7 2.1 %scan.1 = f32[576,128]{1,0:T(8,128)} custom-call(f32[8,128]{1,0:T(8,128)} %reshape.25.decay_ref, f32[1088,128]{1,0:T(8,128)} %bitcast.18), custom_call_target="tpu_custom_call" | custom-call | tf_op jit(solution)/shard_map/scan/pallas_call | solution.py:275
  51.8 6.9 %all-to-all-start.1 = ((f32[64,1,1152]{2,1,0:T(1,128)}), f32[64,1,1152]{2,1,0:T(1,128)S(1)}, u32[]{:S(2)}, u32[]{:S(2)}) async-start(f32[64,1,1152]{2,1,0:T(1,128)} %bitcast.20), calls=%async_computation.1 | async-start | bytes 589824 | tf_op jit(solution)/shard_map/all_to_all | solution.py:280
  58.8 1.2 %copy-done.4 = bf16[1,128,4096]{2,1,0:T(8,128)(2,1)S(1)} copy-done((bf16[1,128,4096]{2,1,0:T(8,128)(2,1)S(1)}, bf16[1,128,4096]{2,1,0:T(8,128)(2,1)}, u32[]{:S(2)}) %copy-start.4) | copy-done | bytes 1048600
  60.0 14.1 %local.1 = (f32[128,4096]{1,0:T(8,128)S(1)}, bf16[128,4096]{1,0:T(8,128)(2,1)S(1)}, bf16[128,4096]{1,0:T(8,128)(2,1)S(1)}) custom-call(f32[16,256]{1,0:T(8,128)S(1)} %copy-done.6, f32[16,256]{1,0:T(8,128)S(1)} %get-tuple-element.9.amp_ref, f32[1,4096]{1,0:T(1,128)S(1)} %reshape.30.rate_row_ref, f32[1,4096]{1,0:T(1,128)S(1)} %reshape.31.amp_row_ref, ...), custom_call_target="tpu_custom_call" | custom-call | flops 8000000000 | bytes 5242880 | tf_op jit(solution)/shard_map/local/pallas_call | solution.py:258
  74.2 1.0 %copy-done = bf16[128,4096]{1,0:T(8,128)(2,1)} copy-done((bf16[128,4096]{1,0:T(8,128)(2,1)}, bf16[128,4096]{1,0:T(8,128)(2,1)S(1)}, u32[]{:S(2)}) %copy-start) | copy-done | bytes 1048600
  75.2 1.8 %collective-permute-start.2 = (f32[64,128]{1,0:T(8,128)S(1)}, f32[64,128]{1,0:T(8,128)S(1)}, u32[]{:S(2)}, u32[]{:S(2)}) collective-permute-start(f32[64,128]{1,0:T(8,128)S(1)} %bitcast.21), channel_id=1, source_target_pairs={{0,192},{64,128},{128,64},{192,0},{1,193},{65,129},{129,65},{193,1... | collective-permute-start | bytes 98312 | tf_op jit(solution)/shard_map/ppermute | solution.py:286
  77.0 1.2 %collective-permute-start.1 = (f32[64,128]{1,0:T(8,128)S(1)}, f32[64,128]{1,0:T(8,128)S(1)}, u32[]{:S(2)}, u32[]{:S(2)}) collective-permute-start(f32[64,128]{1,0:T(8,128)S(1)} %bitcast.22), channel_id=1, source_target_pairs={{0,128},{64,192},{128,0},{192,64},{1,129},{65,193},{129,1},{193,65... | collective-permute-start | bytes 98312 | tf_op jit(solution)/shard_map/ppermute | solution.py:286
  78.2 1.2 %copy-done.1 = bf16[128,4096]{1,0:T(8,128)(2,1)S(1)} copy-done((bf16[128,4096]{1,0:T(8,128)(2,1)S(1)}, bf16[128,4096]{1,0:T(8,128)(2,1)}, u32[]{:S(2)}) %copy-start.1) | copy-done | bytes 1048600
  79.4 4.5 %carry.1 = f32[128,4096]{1,0:T(8,128)} custom-call(f32[576,128]{1,0:T(8,128)S(1)} %bitcast.12, f32[128,4096]{1,0:T(8,128)S(1)} %get-tuple-element.5.local_ref, bf16[128,4096]{1,0:T(8,128)(2,1)S(1)} %get-tuple-element.6.high_ref, bf16[128,4096]{1,0:T(8,128)(2,1)S(1)} %copy-done.1), custom_call_target="tpu_custom_call" | custom-call | flops 800000000 | bytes 7340032 | tf_op jit(solution)/shard_map/carry/pallas_call | solution.py:287
  84.0 0.6 copy-done.11
  84.6 1.8 %finish.1 = f32[16,256]{1,0:T(8,128)} custom-call(f32[16,256]{1,0:T(8,128)} %get-tuple-element.8.factor_ref, f32[64,128]{1,0:T(8,128)} %bitcast.24, f32[64,128]{1,0:T(8,128)} %copy-done.11, f32[64,128]{1,0:T(8,128)} %copy-done.10, f32[64,128]{1,0:T(8,128)} %copy-done.9), custom_call_target="tpu_custom_call" | custom-call | tf_op jit(solution)/shard_map/finish/pallas_call | solution.py:299
  (26 shorter events, 0.2 us)
Async XLA Ops:
  0.6 1.2 %copy-start.2 = (bf16[1,128,4096]{2,1,0:T(8,128)(2,1)S(1)}, bf16[1,128,4096]{2,1,0:T(8,128)(2,1)}, u32[]{:S(2)}) copy-start(bf16[1,128,4096]{2,1,0:T(8,128)(2,1)} %param.5) | copy-start | bytes 3145732
  1.9 1.2 %copy-start.3 = (bf16[1,128,4096]{2,1,0:T(8,128)(2,1)S(1)}, bf16[1,128,4096]{2,1,0:T(8,128)(2,1)}, u32[]{:S(2)}) copy-start(bf16[1,128,4096]{2,1,0:T(8,128)(2,1)} %param.4) | copy-start | bytes 3145732
  3.1 0.7 copy-start.5
  3.8 27.0 %copy-start.6 = (f32[16,256]{1,0:T(8,128)S(1)}, f32[16,256]{1,0:T(8,128)}, u32[]{:S(2)}) copy-start(f32[16,256]{1,0:T(8,128)} %rates_ref.3) | copy-start | bytes 49156
  3.8 27.8 %copy-start.12 = (f32[16,256]{1,0:T(8,128)S(1)}, f32[16,256]{1,0:T(8,128)}, u32[]{:S(2)}) copy-start(f32[16,256]{1,0:T(8,128)} %param.6) | copy-start | bytes 49156
  15.6 33.3 %all-to-all-start = ((f32[64,1,2176]{2,1,0:T(1,128)}), f32[64,1,2176]{2,1,0:T(1,128)S(1)}, u32[]{:S(2)}, u32[]{:S(2)}) async-start(f32[64,1,2176]{2,1,0:T(1,128)} %bitcast.2), calls=%async_computation | async-start | bytes 1114112 | tf_op jit(solution)/shard_map/all_to_all | solution.py:246
  48.9 0.8 copy-start.7
  51.8 23.3 %all-to-all-start.1 = ((f32[64,1,1152]{2,1,0:T(1,128)}), f32[64,1,1152]{2,1,0:T(1,128)S(1)}, u32[]{:S(2)}, u32[]{:S(2)}) async-start(f32[64,1,1152]{2,1,0:T(1,128)} %bitcast.20), calls=%async_computation.1 | async-start | bytes 589824 | tf_op jit(solution)/shard_map/all_to_all | solution.py:280
  58.8 1.2 %copy-start.4 = (bf16[1,128,4096]{2,1,0:T(8,128)(2,1)S(1)}, bf16[1,128,4096]{2,1,0:T(8,128)(2,1)}, u32[]{:S(2)}) copy-start(bf16[1,128,4096]{2,1,0:T(8,128)(2,1)} %param.4) | copy-start | bytes 3145732
  74.2 1.0 %copy-start = (bf16[128,4096]{1,0:T(8,128)(2,1)}, bf16[128,4096]{1,0:T(8,128)(2,1)S(1)}, u32[]{:S(2)}) copy-start(bf16[128,4096]{1,0:T(8,128)(2,1)S(1)} %get-tuple-element.7.low_ref) | copy-start | bytes 3145732
  75.2 8.8 %copy-start.8 = (f32[64,1,128]{2,1,0:T(1,128)}, f32[64,1,128]{2,1,0:T(1,128)S(1)}, u32[]{:S(2)}) copy-start(f32[64,1,128]{2,1,0:T(1,128)S(1)} %slice.4) | copy-start | bytes 98308
  75.2 8.7 %collective-permute-start.2 = (f32[64,128]{1,0:T(8,128)S(1)}, f32[64,128]{1,0:T(8,128)S(1)}, u32[]{:S(2)}, u32[]{:S(2)}) collective-permute-start(f32[64,128]{1,0:T(8,128)S(1)} %bitcast.21), channel_id=1, source_target_pairs={{0,192},{64,128},{128,64},{192,0},{1,193},{65,129},{129,65},{193,1... | collective-permute-start | bytes 98312 | tf_op jit(solution)/shard_map/ppermute | solution.py:286
  77.0 6.9 %collective-permute-start.1 = (f32[64,128]{1,0:T(8,128)S(1)}, f32[64,128]{1,0:T(8,128)S(1)}, u32[]{:S(2)}, u32[]{:S(2)}) collective-permute-start(f32[64,128]{1,0:T(8,128)S(1)} %bitcast.22), channel_id=1, source_target_pairs={{0,128},{64,192},{128,0},{192,64},{1,129},{65,193},{129,1},{193,65... | collective-permute-start | bytes 98312 | tf_op jit(solution)/shard_map/ppermute | solution.py:286
  78.2 5.8 %collective-permute-start = (f32[64,128]{1,0:T(8,128)S(1)}, f32[64,128]{1,0:T(8,128)S(1)}, u32[]{:S(2)}, u32[]{:S(2)}) collective-permute-start(f32[64,128]{1,0:T(8,128)S(1)} %bitcast.23), channel_id=1, source_target_pairs={{0,64},{64,0},{128,192},{192,128},{1,65},{65,1},{129,193},{193,129... | collective-permute-start | bytes 98312 | tf_op jit(solution)/shard_map/ppermute | solution.py:286
  78.2 1.2 %copy-start.1 = (bf16[128,4096]{1,0:T(8,128)(2,1)S(1)}, bf16[128,4096]{1,0:T(8,128)(2,1)}, u32[]{:S(2)}) copy-start(bf16[128,4096]{1,0:T(8,128)(2,1)} %copy-done) | copy-start | bytes 3145732
  83.9 0.6 copy-start.9
  84.0 0.6 copy-start.10
  84.0 0.6 copy-start.11

commit v2 on v1

v2 whole, which is shorter than its diff:
```python
import functools

import jax
import jax.numpy as jnp
from jax import lax
from jax.experimental import pallas as pl
from jax.experimental.pallas import tpu as pltpu
from jax.sharding import Mesh
from jax.sharding import PartitionSpec as P

CTX = ("ctx_0", "ctx_1", "ctx_2")
LANES = 128
CG = 16
GT = LANES // CG
SUB = 16
STEPS = 4
F32 = jnp.float32
BF16 = jnp.bfloat16
HIGHEST = lax.Precision.HIGHEST


def iota(shape, dim):
    return lax.broadcasted_iota(jnp.int32, shape, dim)


def split(value):
    high = value.astype(BF16)
    return high, (value - high.astype(F32)).astype(BF16)


def dot(a, b, dims=((1,), (0,))):
    return lax.dot_general(a, b, (dims, ((), ())), preferred_element_type=F32)


def group_columns(table, first):
    groups = table.shape[1]
    turned = pltpu.roll(table, (groups - first) % groups, 1)
    return [jnp.broadcast_to(turned[:, g : g + 1], (table.shape[0], LANES)) for g in range(GT)]


def own_group(full, rows):
    group_of = iota((rows, LANES), 1) // CG
    kept = full[:rows]
    for g in range(1, GT):
        kept = jnp.where(group_of == g, full[g * rows : (g + 1) * rows], kept)
    return kept


def on_diagonal(part):
    group_of = iota(part.shape, 1) // CG
    zero = jnp.zeros_like(part)
    return jnp.concatenate([jnp.where(group_of == g, part, zero) for g in range(GT)], 0)


def windows(piece):
    shifted = [piece]
    for first in range(SUB, piece.shape[0], SUB):
        shifted.append(jnp.concatenate([piece[first:], jnp.zeros((first, LANES), BF16)], 0))
    return jnp.concatenate(shifted, 1)


def mode_rows(table):
    modes, groups = table.shape
    pick = (iota((modes, LANES), 0) == iota((modes, LANES), 1) % CG).astype(F32)
    spread = lax.dot_general(
        table, pick, (((0,), (0,)), ((), ())), precision=HIGHEST, preferred_element_type=F32
    ).reshape(groups // GT, GT, LANES)
    keep = iota((GT, LANES), 0) == iota((GT, LANES), 1) // CG
    return jnp.sum(jnp.where(keep[None], spread, 0.0), axis=1)


def summary_kernel(
    rates_hbm, grad_hbm, in_hbm, out_hbm, rates_ref, grad_ref, in_ref, sent_ref, pair_ref, sems, sent_sems
):
    rows, width = grad_ref.shape
    modes = rates_ref.shape[0]
    half = modes // 2
    all_tiles = width // LANES
    tiles = all_tiles // STEPS
    block = tiles * LANES
    chunk = tiles * 17
    loads = [pltpu.make_async_copy(rates_hbm, rates_ref, sems.at[0])]
    for q in range(STEPS):
        at = pl.ds(q * block, block)
        for i, (source, into) in enumerate(((grad_hbm, grad_ref), (in_hbm, in_ref))):
            loads.append(
                pltpu.make_async_copy(source.at[:, at], into.at[:, at], sems.at[1 + 2 * q + i])
            )
    for load in loads:
        load.start()
    pos = iota((modes, LANES), 1).astype(F32)
    step = iota((SUB, LANES), 0).astype(F32)
    later = iota((GT, SUB, LANES), 2) >= iota((GT, SUB, LANES), 1)
    later = later.reshape(GT * SUB, LANES)
    loads[0].wait()
    rates = rates_ref[...]
    rate_rows = mode_rows(rates)

    def pair_tile(tile):
        at = pl.ds(tile * LANES, LANES)
        inp = in_ref[:, at]
        left = jnp.concatenate(
            [on_diagonal(inp[i : i + SUB]) for i in range(0, rows, SUB)], 1
        )
        pairs = dot(left, windows(grad_ref[:, at]), ((1,), (1,)))
        high, low = split(jnp.where(later, pairs, 0.0))
        pair_ref[tile, :, :LANES] = high
        pair_ref[tile, :, LANES:] = low

    def one_tile(tile):
        at = pl.ds(tile * LANES, LANES)
        grad = grad_ref[:, at]
        inp = in_ref[:, at]
        columns = group_columns(rates, tile * GT)
        high, low = split(jnp.concatenate([jnp.exp(-r * pos) for r in columns], 0))
        left = jnp.concatenate([high, low], 1)
        summary = own_group(dot(left, jnp.concatenate([grad, grad], 0)), modes)
        tails = jnp.concatenate([jnp.exp(-r * (rows - pos)) for r in columns], 0)
        left = jnp.concatenate(split(tails), 1)
        tail = own_group(dot(left, jnp.concatenate([inp, inp], 0)), modes)
        pairs = pair_ref[tile]
        weighted = dot(
            jnp.concatenate([pairs, pairs[:, :LANES]], 1),
            jnp.concatenate([high, high, low], 1),
            ((1,), (1,)),
        )
        growth = jnp.exp(rate_rows[tile : tile + 1] * step)
        cells = jnp.sum(own_group(weighted, SUB) * growth, axis=0, keepdims=True)
        for a in range(2):
            base = (a * all_tiles + tile) * 17
            sent_ref[base : base + 8, :] = summary[a * half : (a + 1) * half]
            sent_ref[base + 8 : base + 16, :] = tail[a * half : (a + 1) * half]
            sent_ref[base + 16 : base + 17, :] = cells

    stores = []
    for q in range(STEPS):
        loads[1 + 2 * q].wait()
        loads[2 + 2 * q].wait()
        for tile in range(q * tiles, (q + 1) * tiles):
            pair_tile(tile)
        for tile in range(q * tiles, (q + 1) * tiles):
            one_tile(tile)
        for a in range(2):
            at = pl.ds((a * STEPS + q) * chunk, chunk)
            stores.append(
                pltpu.make_async_copy(
                    sent_ref.at[at], out_hbm.at[at], sent_sems.at[a * STEPS + q]
                )
            )
            stores[-1].start()
    for store in stores:
        store.wait()


def local_kernel(rates_ref, rate_row_ref, amp_row_ref, grad_ref, out_ref, weight_ref):
    rows = grad_ref.shape[0]
    modes = rates_ref.shape[0]
    tiles = grad_ref.shape[1] // LANES
    pos = iota((modes, LANES), 1).astype(F32)
    step = iota((SUB, LANES), 0).astype(F32)
    later = iota((GT, SUB, LANES), 2) >= iota((GT, SUB, LANES), 1)
    later = later.reshape(GT * SUB, LANES)
    to_end = (rows - iota((rows, LANES), 0)).astype(F32)

    def one_tile(k, carry):
        tile = pl.program_id(0) * tiles + k
        at = pl.ds(pl.multiple_of(k * LANES, LANES), LANES)
        grad = grad_ref[:, at]
        columns = group_columns(rates_ref[...], tile * GT)
        high, low = split(jnp.concatenate([jnp.exp(-r * pos) for r in columns], 0))
        amp_row = amp_row_ref[:, at]
        rate_row = rate_row_ref[:, at]
        grown = [on_diagonal(part) for part in split(amp_row * jnp.exp(rate_row * step))]
        kernel = dot(
            jnp.concatenate([grown[0], grown[1], grown[0]], 1),
            jnp.concatenate([high, high, low], 0),
        )
        left = jnp.concatenate(split(jnp.where(later, kernel, 0.0)), 1)
        wide = windows(grad)
        full = dot(left, jnp.concatenate([wide, wide], 0))
        for i in range(rows // SUB):
            out_ref[i * SUB : (i + 1) * SUB, at] = own_group(
                full[:, i * LANES : (i + 1) * LANES], SUB
            )
        high, low = split(amp_row * jnp.exp(-rate_row * to_end))
        weight_ref[:rows, at] = high
        weight_ref[rows:, at] = low
        return carry

    lax.fori_loop(0, tiles, one_tile, 0, unroll=8)


def scan_kernel(half_ref, decay_ref, in_ref, out_ref):
    shards = in_ref.shape[0] // 17
    decay = decay_ref[...]
    state = jnp.zeros((8, LANES), F32)
    total = jnp.zeros((8, LANES), F32)
    row = jnp.zeros((1, LANES), F32)
    for j in reversed(range(shards)):
        out_ref[9 * j : 9 * j + 8, :] = state
        total = total + in_ref[17 * j + 8 : 17 * j + 16, :] * state
        row = row + in_ref[17 * j + 16 : 17 * j + 17, :]
        state = in_ref[17 * j : 17 * j + 8, :] + decay * state
    same = iota((LANES, LANES), 0) // CG == iota((LANES, LANES), 1) // CG
    summed = lax.dot_general(
        total,
        same.astype(F32),
        (((1,), (0,)), ((), ())),
        precision=HIGHEST,
        preferred_element_type=F32,
    )
    place = iota((8, LANES), 1) % CG == iota((8, LANES), 0) + half_ref[0]
    row = row + jnp.sum(jnp.where(place, summed, 0.0), axis=0, keepdims=True)
    for j in range(shards):
        out_ref[9 * j + 8 : 9 * j + 9, :] = row


def carry_kernel(state_ref, local_ref, weight_ref, out_hbm, out_ref, sems):
    rows, width = out_ref.shape
    all_tiles = width // LANES
    block = width // STEPS
    stores = []
    for tile in range(all_tiles):
        at = pl.ds(tile * LANES, LANES)
        state = jnp.concatenate(
            [state_ref[pl.ds((a * all_tiles + tile) * 9, 8), :] for a in range(2)], 0
        )
        rights = [on_diagonal(part) for part in split(state)]
        high = weight_ref[:rows, at]
        left = jnp.concatenate([high, weight_ref[rows:, at], high], 1)
        right = jnp.concatenate([rights[0], rights[0], rights[1]], 0)
        out_ref[:, at] = local_ref[:, at] + dot(left, right)
        if (tile + 1) % (all_tiles // STEPS) == 0:
            q = tile // (all_tiles // STEPS)
            at = pl.ds(q * block, block)
            stores.append(
                pltpu.make_async_copy(out_ref.at[:, at], out_hbm.at[:, at], sems.at[q])
            )
            stores[-1].start()
    for store in stores:
        store.wait()


def finish_kernel(factor_ref, a_ref, b_ref, c_ref, d_ref, out_ref):
    total = (a_ref[...] + b_ref[...]) + (c_ref[...] + d_ref[...])
    count = total.shape[0] // 2
    modes, groups = out_ref.shape
    early = iota((count, LANES), 1) % CG < modes // 2
    total = jnp.where(early, total[:count], total[count:])
    pick = (iota((count, groups), 0) == iota((count, groups), 1) // GT).astype(F32)
    keep = iota((GT, CG, groups), 0) == iota((GT, CG, groups), 2) % GT
    spread = lax.dot_general(
        total, pick, (((0,), (0,)), ((), ())), precision=HIGHEST, preferred_element_type=F32
    ).reshape(GT, CG, groups)
    out_ref[...] = jnp.sum(jnp.where(keep, spread, 0.0), axis=0) * factor_ref[...]


def whole(shape):
    return pl.BlockSpec(shape, lambda *_: (0,) * len(shape))


def local(grad_out, inputs, residues, rates):
    _, rows, width = grad_out.shape
    modes, groups = residues.shape
    tiles = width // LANES
    shards = lax.axis_size(CTX)
    seqs = lax.axis_size("seq_x") * lax.axis_size("seq_core")
    block = width // STEPS
    slab = pl.BlockSpec((rows, block), lambda q: (0, q))
    anywhere = pl.BlockSpec(memory_space=pl.ANY)
    grad = grad_out[0]
    inp = inputs[0]
    full = pltpu.CompilerParams(vmem_limit_bytes=60 * 1024 * 1024)
    vmem = pltpu.CompilerParams(vmem_limit_bytes=16 * 1024 * 1024)
    small = pltpu.CompilerParams(vmem_limit_bytes=8 * 1024 * 1024)

    sent = pl.pallas_call(
        summary_kernel,
        in_specs=[anywhere, anywhere, anywhere],
        out_specs=anywhere,
        out_shape=jax.ShapeDtypeStruct((shards * 17, LANES), F32),
        scratch_shapes=[
            pltpu.VMEM((modes, groups), F32),
            pltpu.VMEM((rows, width), BF16),
            pltpu.VMEM((rows, width), BF16),
            pltpu.VMEM((shards * 17, LANES), F32),
            pltpu.VMEM((tiles, LANES, 2 * LANES), BF16),
            pltpu.SemaphoreType.DMA((1 + 2 * STEPS,)),
            pltpu.SemaphoreType.DMA((2 * STEPS,)),
        ],
        compiler_params=full,
        name="summary",
    )(rates, grad, inp)
    got = lax.all_to_all(sent.reshape(shards, 1, 17 * LANES), CTX, 0, 0, tiled=True)

    amplitude = residues * jnp.sqrt(-jnp.expm1(-2.0 * rates) / modes)
    factor = jnp.sqrt(-jnp.expm1(-2.0 * rates) / float(seqs * shards * rows * (width // groups)))
    place = lax.axis_index(CTX)
    half = modes // 2
    first_mode = place // tiles * half
    own_rates = lax.dynamic_slice(rates, (first_mode, place % tiles * GT), (half, GT))
    decay = jnp.repeat(jnp.exp(-own_rates * rows), CG, axis=1)

    row = pl.BlockSpec((1, block), lambda q: (0, q))
    local_in, weight = pl.pallas_call(
        local_kernel,
        grid=(STEPS,),
        in_specs=[whole((modes, groups)), row, row, slab],
        out_specs=[slab, pl.BlockSpec((2 * rows, block), lambda q: (0, q))],
        out_shape=[
            jax.ShapeDtypeStruct((rows, width), F32),
            jax.ShapeDtypeStruct((2 * rows, width), BF16),
        ],
        compiler_params=vmem,
        name="local",
        cost_estimate=pl.CostEstimate(
            flops=8 * 10**9, bytes_accessed=5 * 2**20, transcendentals=10**6
        ),
    )(rates, rates.T.reshape(1, width), amplitude.T.reshape(1, width), grad)

    got, local_in = lax.optimization_barrier((got, local_in))
    states = pl.pallas_call(
        scan_kernel,
        in_specs=[
            pl.BlockSpec(memory_space=pltpu.SMEM),
            whole((half, LANES)),
            whole((shards * 17, LANES)),
        ],
        out_shape=jax.ShapeDtypeStruct((shards * 9, LANES), F32),
        compiler_params=small,
        name="scan",
    )(first_mode[None], decay, got.reshape(shards * 17, LANES))
    back = lax.all_to_all(states.reshape(shards, 1, 9 * LANES), CTX, 0, 0, tiled=True)

    mine = back[:, 0, 8 * LANES :]
    others = [mine]
    for bits in (1, 2, 3):
        pairs = [(d, d ^ bits) for d in range(4)]
        others.append(lax.ppermute(mine, ("seq_x", "seq_core"), pairs))
    grad_in = pl.pallas_call(
        carry_kernel,
        in_specs=[whole((shards * 9, LANES)), whole((rows, width)), whole((2 * rows, width))],
        out_specs=anywhere,
        out_shape=jax.ShapeDtypeStruct((rows, width), F32),
        scratch_shapes=[pltpu.VMEM((rows, width), F32), pltpu.SemaphoreType.DMA((STEPS,))],
        compiler_params=vmem,
        name="carry",
        cost_estimate=pl.CostEstimate(
            flops=8 * 10**8, bytes_accessed=7 * 2**20, transcendentals=0
        ),
    )(back.reshape(shards * 9, LANES), local_in, weight)
    grad_res = pl.pallas_call(
        finish_kernel,
        out_shape=jax.ShapeDtypeStruct((modes, groups), F32),
        compiler_params=small,
        name="finish",
    )(factor, *others)
    return grad_in[None], grad_res


def solution(mesh):
    torus = Mesh(
        mesh.devices.reshape(2, 2, 2, 8, 4), ("seq_x", "seq_core", "ctx_0", "ctx_1", "ctx_2")
    )
    seq = ("seq_x", "seq_core")
    return jax.shard_map(
        local,
        mesh=torus,
        in_specs=(P(seq, CTX, None), P(seq, CTX, None), P(), P()),
        out_specs=(P(seq, CTX, None), P()),
        check_vma=False,
    )
```

time: 87 us -> 70.5 us (0.81)
  blocking collectives: 0 us -> 19.1 us
  Pallas kernels: 34.4 us -> 18.7 us
  waiting for transfers between devices: 16.3 us -> 6.28 us
  starting transfers between devices: 25.1 us -> 20.5 us
  local copies, waits for them, and re-layouts: 9.19 us -> 4.74 us
    all_to_all x0 -> x1, blocking collectives: none -> 19.1 us  [local(): lax.all_to_all(states.reshape(shards, 1, 9 * LANES), CTX, 0, 0, tiled=True)]
    pallas_call x4, Pallas kernels: 32.5 us -> 17.8 us  [the longest x1 8.63 us: local(): pl.pallas_call(local_kernel, grid=(STEPS,), in_specs=[whole((modes, group...]
    all_to_all x1, waiting for transfers between devices: 16.3 us -> 6.27 us  [local(): lax.all_to_all(sent.reshape(shards, 1, 17 * LANES), CTX, 0, 0, tiled=True)]
    all_to_all x1 -> x0, starting transfers between devices: 6.94 us -> none  [local(): lax.all_to_all(states.reshape(shards, 1, 9 * LANES), CTX, 0, 0, tiled=True)]
    unnamed x26 -> x10, local copies, waits for them, and re-layouts: 7.98 us -> 4.13 us
    ppermute x3, starting transfers between devices: 3.02 us -> 5.35 us  [local(): others.append(lax.ppermute(mine, ('seq_x', 'seq_core'), pairs))]
    pallas_call x1, Pallas kernels: 1.85 us -> 0.92 us  [local(): pl.pallas_call(finish_kernel, out_shape=jax.ShapeDtypeStruct((modes, grou...]
  transfers between devices with their start and end apart: 5 -> 4, of which waited for: 1 -> 1; matrix products, arithmetic and copies ran while one was open for 2% -> 1% of each run, Pallas kernels for 22% -> 15%
where the time goes in v2:
time: 70.5 us; the launch traced here: 70.2 us
  starting transfers between devices  20.5 us (29%)
  blocking collectives  19.1 us (27%)
  Pallas kernels  18.7 us (27%)
  waiting for transfers between devices  6.28 us (9%)
  local copies, waits for them, and re-layouts  4.74 us (7%)
  between operations  0.8 us (1%)
    all_to_all x1, blocking collectives, local(): lax.all_to_all(states.reshape(shards, 1, 9 * LANES), CTX, 0, 0, tiled=True)  19.1 us
    all_to_all x1, starting transfers between devices, local(): lax.all_to_all(sent.reshape(shards, 1, 17 * LANES), CTX, 0, 0, tiled=True)  15.1 us
    pallas_call x1, Pallas kernels, local(): pl.pallas_call(local_kernel, grid=(STEPS,), in_specs=[whole((modes, group...  8.63 us
    pallas_call x1, Pallas kernels, local(): pl.pallas_call(summary_kernel, in_specs=[anywhere, anywhere, anywhere], o...  7 us
    all_to_all x1, waiting for transfers between devices, local(): lax.all_to_all(sent.reshape(shards, 1, 17 * LANES), CTX, 0, 0, tiled=True)  6.27 us
    ppermute x3, starting transfers between devices, local(): others.append(lax.ppermute(mine, ('seq_x', 'seq_core'), pairs))  5.35 us
    unnamed x10, local copies, waits for them, and re-layouts  4.13 us
    pallas_call x1, Pallas kernels, local(): pl.pallas_call(carry_kernel, in_specs=[whole((shards * 9, LANES)), whole(...  1.82 us
  transfers between devices with their start and end apart: 4, of which 1 were waited for; matrix products, arithmetic and copies ran while one was open for 1% of the time, Pallas kernels for 15%

profile of v2, /device:TPU:1, one launch (start us, length us, event | category | flops | bytes accessed | tf_op | source)
XLA Modules:
  0.0 70.2 jit_solution(1388257499904568463)
XLA Ops:
  0.7 7.0 %summary.1 = f32[1088,128]{1,0:T(8,128)} custom-call(f32[16,256]{1,0:T(8,128)} %rates_ref.1, bf16[128,4096]{1,0:T(8,128)(2,1)} %bitcast.17, bf16[128,4096]{1,0:T(8,128)(2,1)} %bitcast.26), custom_call_target="tpu_custom_call" | custom-call | tf_op jit(solution)/shard_map/summary/pallas_call | solution.py:277
  7.7 15.1 %all-to-all-start = ((f32[64,1,2176]{2,1,0:T(1,128)}), f32[64,1,2176]{2,1,0:T(1,128)S(1)}, u32[]{:S(2)}, u32[]{:S(2)}) async-start(f32[64,1,2176]{2,1,0:T(1,128)} %bitcast.24), calls=%async_computation | async-start | bytes 1114112 | tf_op jit(solution)/shard_map/all_to_all | solution.py:294
  22.8 0.1 multiply_exponential_fusion
  22.9 0.1 broadcast_in_dim.10
  23.0 0.1 reshape.25.decay_ref
  23.1 0.1 copy.11
  23.2 0.1 reshape.28.amp_row_ref
  23.3 0.1 copy.10
  23.4 0.1 reshape.27.rate_row_ref
  23.5 0.0 copy-start.2
  23.6 1.2 %copy-done.2 = bf16[1,128,4096]{2,1,0:T(8,128)(2,1)S(1)} copy-done((bf16[1,128,4096]{2,1,0:T(8,128)(2,1)S(1)}, bf16[1,128,4096]{2,1,0:T(8,128)(2,1)}, u32[]{:S(2)}) %copy-start.2) | copy-done | bytes 1048600
  24.8 8.6 %local.1 = (f32[128,4096]{1,0:T(8,128)S(1)}, bf16[256,4096]{1,0:T(8,128)(2,1)S(1)}) custom-call(f32[16,256]{1,0:T(8,128)S(1)} %copy-done.3, f32[1,4096]{1,0:T(1,128)S(1)} %reshape.27.rate_row_ref, f32[1,4096]{1,0:T(1,128)S(1)} %reshape.28.amp_row_ref, bf16[128,4096]{1,0:T(8,128)(2,1)S(1)} %bitcast.18), custom_call_target="tpu_custom_call" | custom-call | flops 8000000000 | bytes 5242880 | tf_op jit(solution)/shard_map/local/pallas_call | solution.py:305
  33.4 0.0 copy-start
  33.4 1.3 %copy-done = bf16[256,4096]{1,0:T(8,128)(2,1)} copy-done((bf16[256,4096]{1,0:T(8,128)(2,1)}, bf16[256,4096]{1,0:T(8,128)(2,1)S(1)}, u32[]{:S(2)}) %copy-start) | copy-done | bytes 2097176
  34.7 6.3 %all-to-all-done = f32[64,1,2176]{2,1,0:T(1,128)S(1)} async-done(((f32[64,1,2176]{2,1,0:T(1,128)}), f32[64,1,2176]{2,1,0:T(1,128)S(1)}, u32[]{:S(2)}, u32[]{:S(2)}) %all-to-all-start) | async-done | bytes 557088 | tf_op jit(solution)/shard_map/all_to_all | solution.py:294
  41.0 0.3 scan.1
  41.3 19.1 %all_to_all.10 = f32[64,1,1152]{2,1,0:T(1,128)S(1)} all-to-all(f32[64,1,1152]{2,1,0:T(1,128)S(1)} %bitcast.16), channel_id=1, replica_groups=mesh['seq_x'=2,'seq_core'=2,'ctx_0'=2,'ctx_1'=8,'ctx_2'=4] {'ctx_0','ctx..., dimensions={0} | all-to-all | bytes 589824 | tf_op jit(solution)/shard_map/all_to_all | solution.py:333
  60.5 4.2 %collective-permute-start.2 = (f32[64,128]{1,0:T(8,128)S(1)}, f32[64,128]{1,0:T(8,128)S(1)}, u32[]{:S(2)}, u32[]{:S(2)}) collective-permute-start(f32[64,128]{1,0:T(8,128)S(1)} %bitcast.20), channel_id=1, source_target_pairs={{0,192},{64,128},{128,64},{192,0},{1,193},{65,129},{129,65},{193,1... | collective-permute-start | bytes 98312 | tf_op jit(solution)/shard_map/ppermute | solution.py:339
  64.7 1.2 %collective-permute-start.1 = (f32[64,128]{1,0:T(8,128)S(1)}, f32[64,128]{1,0:T(8,128)S(1)}, u32[]{:S(2)}, u32[]{:S(2)}) collective-permute-start(f32[64,128]{1,0:T(8,128)S(1)} %bitcast.21), channel_id=1, source_target_pairs={{0,128},{64,192},{128,0},{192,64},{1,129},{65,193},{129,1},{193,65... | collective-permute-start | bytes 98312 | tf_op jit(solution)/shard_map/ppermute | solution.py:339
  65.8 0.0 collective-permute-start
  65.8 1.6 %copy-done.1 = bf16[256,4096]{1,0:T(8,128)(2,1)S(1)} copy-done((bf16[256,4096]{1,0:T(8,128)(2,1)S(1)}, bf16[256,4096]{1,0:T(8,128)(2,1)}, u32[]{:S(2)}) %copy-start.1) | copy-done | bytes 2097176
  67.4 1.8 %carry.1 = f32[128,4096]{1,0:T(8,128)} custom-call(f32[576,128]{1,0:T(8,128)S(1)} %bitcast.15, f32[128,4096]{1,0:T(8,128)S(1)} %get-tuple-element.8.local_ref, bf16[256,4096]{1,0:T(8,128)(2,1)S(1)} %copy-done.1), custom_call_target="tpu_custom_call" | custom-call | flops 800000000 | bytes 7340032 | tf_op jit(solution)/shard_map/carry/pallas_call | solution.py:340
  69.2 0.0 collective-permute-done.2.d_ref
  69.3 0.9 %finish.1 = f32[16,256]{1,0:T(8,128)} custom-call(f32[16,256]{1,0:T(8,128)S(1)} %get-tuple-element.10.factor_ref, f32[64,128]{1,0:T(8,128)S(1)} %bitcast.23, f32[64,128]{1,0:T(8,128)S(1)} %collective-permute-done.b_ref, f32[64,128]{1,0:T(8,128)S(1)} %collective-permute-done.1.c_ref, f32[64,128]{1,0:T(8,128)S(1)} %collective-permute-done.2.d_ref), custom_call_target="tpu_custom_call" | custom-call | tf_op jit(solution)/shard_map/finish/pallas_call | solution.py:352
  (9 shorter events, 0.1 us)
Async XLA Ops:
  0.6 22.2 %copy-start.3 = (f32[16,256]{1,0:T(8,128)S(1)}, f32[16,256]{1,0:T(8,128)}, u32[]{:S(2)}) copy-start(f32[16,256]{1,0:T(8,128)} %rates_ref.1) | copy-start | bytes 49156
  0.6 22.4 %copy-start.4 = (f32[16,256]{1,0:T(8,128)S(1)}, f32[16,256]{1,0:T(8,128)}, u32[]{:S(2)}) copy-start(f32[16,256]{1,0:T(8,128)} %param.6) | copy-start | bytes 49156
  7.7 33.3 %all-to-all-start = ((f32[64,1,2176]{2,1,0:T(1,128)}), f32[64,1,2176]{2,1,0:T(1,128)S(1)}, u32[]{:S(2)}, u32[]{:S(2)}) async-start(f32[64,1,2176]{2,1,0:T(1,128)} %bitcast.24), calls=%async_computation | async-start | bytes 1114112 | tf_op jit(solution)/shard_map/all_to_all | solution.py:294
  23.5 1.2 %copy-start.2 = (bf16[1,128,4096]{2,1,0:T(8,128)(2,1)S(1)}, bf16[1,128,4096]{2,1,0:T(8,128)(2,1)}, u32[]{:S(2)}) copy-start(bf16[1,128,4096]{2,1,0:T(8,128)(2,1)} %param.4) | copy-start | bytes 3145732
  33.4 1.3 %copy-start = (bf16[256,4096]{1,0:T(8,128)(2,1)}, bf16[256,4096]{1,0:T(8,128)(2,1)S(1)}, u32[]{:S(2)}) copy-start(bf16[256,4096]{1,0:T(8,128)(2,1)S(1)} %get-tuple-element.9.weight_ref) | copy-start | bytes 6291460
  60.5 8.8 %collective-permute-start.2 = (f32[64,128]{1,0:T(8,128)S(1)}, f32[64,128]{1,0:T(8,128)S(1)}, u32[]{:S(2)}, u32[]{:S(2)}) collective-permute-start(f32[64,128]{1,0:T(8,128)S(1)} %bitcast.20), channel_id=1, source_target_pairs={{0,192},{64,128},{128,64},{192,0},{1,193},{65,129},{129,65},{193,1... | collective-permute-start | bytes 98312 | tf_op jit(solution)/shard_map/ppermute | solution.py:339
  64.7 4.6 %collective-permute-start.1 = (f32[64,128]{1,0:T(8,128)S(1)}, f32[64,128]{1,0:T(8,128)S(1)}, u32[]{:S(2)}, u32[]{:S(2)}) collective-permute-start(f32[64,128]{1,0:T(8,128)S(1)} %bitcast.21), channel_id=1, source_target_pairs={{0,128},{64,192},{128,0},{192,64},{1,129},{65,193},{129,1},{193,65... | collective-permute-start | bytes 98312 | tf_op jit(solution)/shard_map/ppermute | solution.py:339
  65.8 3.4 %collective-permute-start = (f32[64,128]{1,0:T(8,128)S(1)}, f32[64,128]{1,0:T(8,128)S(1)}, u32[]{:S(2)}, u32[]{:S(2)}) collective-permute-start(f32[64,128]{1,0:T(8,128)S(1)} %bitcast.22), channel_id=1, source_target_pairs={{0,64},{64,0},{128,192},{192,128},{1,65},{65,1},{129,193},{193,129... | collective-permute-start | bytes 98312 | tf_op jit(solution)/shard_map/ppermute | solution.py:339
  65.8 1.6 %copy-start.1 = (bf16[256,4096]{1,0:T(8,128)(2,1)S(1)}, bf16[256,4096]{1,0:T(8,128)(2,1)}, u32[]{:S(2)}) copy-start(bf16[256,4096]{1,0:T(8,128)(2,1)} %copy-done) | copy-start | bytes 6291460

commit v3 on v2

--- a/solution.py
+++ b/solution.py
@@ -1,5 +1,3 @@
-import functools
-
 import jax
 import jax.numpy as jnp
 from jax import lax
@@ -14,6 +12,7 @@
 GT = LANES // CG
 SUB = 16
 STEPS = 4
+HALVES = 2
 F32 = jnp.float32
 BF16 = jnp.bfloat16
 HIGHEST = lax.Precision.HIGHEST
@@ -59,14 +58,13 @@
     return jnp.concatenate(shifted, 1)
 
 
-def mode_rows(table):
-    modes, groups = table.shape
-    pick = (iota((modes, LANES), 0) == iota((modes, LANES), 1) % CG).astype(F32)
-    spread = lax.dot_general(
-        table, pick, (((0,), (0,)), ((), ())), precision=HIGHEST, preferred_element_type=F32
-    ).reshape(groups // GT, GT, LANES)
-    keep = iota((GT, LANES), 0) == iota((GT, LANES), 1) // CG
-    return jnp.sum(jnp.where(keep[None], spread, 0.0), axis=1)
+def mode_row(columns):
+    modes = columns[0].shape[0]
+    ahead = iota((modes, LANES), 1) - iota((modes, LANES), 0)
+    placed = jnp.where(ahead == 0, columns[0], 0.0)
+    for g in range(1, GT):
+        placed = jnp.where(ahead == g * CG, columns[g], placed)
+    return jnp.sum(placed, axis=0, keepdims=True)
 
 
 def summary_kernel(
@@ -76,11 +74,11 @@
     modes = rates_ref.shape[0]
     half = modes // 2
     all_tiles = width // LANES
-    tiles = all_tiles // STEPS
+    tiles = all_tiles // HALVES
     block = tiles * LANES
     chunk = tiles * 17
     loads = [pltpu.make_async_copy(rates_hbm, rates_ref, sems.at[0])]
-    for q in range(STEPS):
+    for q in range(HALVES):
         at = pl.ds(q * block, block)
         for i, (source, into) in enumerate(((grad_hbm, grad_ref), (in_hbm, in_ref))):
             loads.append(
@@ -92,9 +90,6 @@
     step = iota((SUB, LANES), 0).astype(F32)
     later = iota((GT, SUB, LANES), 2) >= iota((GT, SUB, LANES), 1)
     later = later.reshape(GT * SUB, LANES)
-    loads[0].wait()
-    rates = rates_ref[...]
-    rate_rows = mode_rows(rates)
 
     def pair_tile(tile):
         at = pl.ds(tile * LANES, LANES)
@@ -107,7 +102,7 @@
         pair_ref[tile, :, :LANES] = high
         pair_ref[tile, :, LANES:] = low
 
-    def one_tile(tile):
+    def one_tile(tile, rates):
         at = pl.ds(tile * LANES, LANES)
         grad = grad_ref[:, at]
         inp = in_ref[:, at]
@@ -124,7 +119,7 @@
             jnp.concatenate([high, high, low], 1),
             ((1,), (1,)),
         )
-        growth = jnp.exp(rate_rows[tile : tile + 1] * step)
+        growth = jnp.exp(mode_row(columns) * step)
         cells = jnp.sum(own_group(weighted, SUB) * growth, axis=0, keepdims=True)
         for a in range(2):
             base = (a * all_tiles + tile) * 17
@@ -132,19 +127,31 @@
             sent_ref[base + 8 : base + 16, :] = tail[a * half : (a + 1) * half]
             sent_ref[base + 16 : base + 17, :] = cells
 
-    stores = []
-    for q in range(STEPS):
+    def arrived(q):
         loads[1 + 2 * q].wait()
         loads[2 + 2 * q].wait()
-        for tile in range(q * tiles, (q + 1) * tiles):
-            pair_tile(tile)
-        for tile in range(q * tiles, (q + 1) * tiles):
-            one_tile(tile)
+
+    def of_step(q):
+        return range(q * tiles, (q + 1) * tiles)
+
+    arrived(0)
+    for tile in of_step(0):
+        pair_tile(tile)
+    loads[0].wait()
+    rates = rates_ref[...]
+    stores = []
+    for q in range(HALVES):
+        if q + 1 < HALVES:
+            arrived(q + 1)
+            for tile in of_step(q + 1):
+                pair_tile(tile)
+        for tile in of_step(q):
+            one_tile(tile, rates)
         for a in range(2):
-            at = pl.ds((a * STEPS + q) * chunk, chunk)
+            at = pl.ds((a * HALVES + q) * chunk, chunk)
             stores.append(
                 pltpu.make_async_copy(
-                    sent_ref.at[at], out_hbm.at[at], sent_sems.at[a * STEPS + q]
+                    sent_ref.at[at], out_hbm.at[at], sent_sems.at[a * HALVES + q]
                 )
             )
             stores[-1].start()
@@ -152,7 +159,7 @@
         store.wait()
 
 
-def local_kernel(rates_ref, rate_row_ref, amp_row_ref, grad_ref, out_ref, weight_ref):
+def local_kernel(rates_ref, rate_row_ref, amp_row_ref, grad_ref, out_ref, near_ref, far_ref):
     rows = grad_ref.shape[0]
     modes = rates_ref.shape[0]
     tiles = grad_ref.shape[1] // LANES
@@ -160,7 +167,9 @@
     step = iota((SUB, LANES), 0).astype(F32)
     later = iota((GT, SUB, LANES), 2) >= iota((GT, SUB, LANES), 1)
     later = later.reshape(GT * SUB, LANES)
-    to_end = (rows - iota((rows, LANES), 0)).astype(F32)
+    blocks = rows // SUB
+    to_next = (SUB - iota((SUB, LANES), 0)).astype(F32)
+    to_end = (SUB * (blocks - 1 - iota((blocks, LANES), 0))).astype(F32)
 
     def one_tile(k, carry):
         tile = pl.program_id(0) * tiles + k
@@ -182,9 +191,8 @@
             out_ref[i * SUB : (i + 1) * SUB, at] = own_group(
                 full[:, i * LANES : (i + 1) * LANES], SUB
             )
-        high, low = split(amp_row * jnp.exp(-rate_row * to_end))
-        weight_ref[:rows, at] = high
-        weight_ref[rows:, at] = low
+        near_ref[:, at] = amp_row * jnp.exp(-rate_row * to_next)
+        far_ref[:, at] = jnp.exp(-rate_row * to_end)
         return carry
 
     lax.fori_loop(0, tiles, one_tile, 0, unroll=8)
@@ -215,7 +223,7 @@
         out_ref[9 * j + 8 : 9 * j + 9, :] = row
 
 
-def carry_kernel(state_ref, local_ref, weight_ref, out_hbm, out_ref, sems):
+def carry_kernel(state_ref, local_ref, near_ref, far_ref, out_hbm, out_ref, sems):
     rows, width = out_ref.shape
     all_tiles = width // LANES
     block = width // STEPS
@@ -226,8 +234,12 @@
             [state_ref[pl.ds((a * all_tiles + tile) * 9, 8), :] for a in range(2)], 0
         )
         rights = [on_diagonal(part) for part in split(state)]
-        high = weight_ref[:rows, at]
-        left = jnp.concatenate([high, weight_ref[rows:, at], high], 1)
+        near = near_ref[:, at]
+        far = far_ref[:, at]
+        high, low = split(
+            jnp.concatenate([near * far[i : i + 1] for i in range(rows // SUB)], 0)
+        )
+        left = jnp.concatenate([high, low, high], 1)
         right = jnp.concatenate([rights[0], rights[0], rights[1]], 0)
         out_ref[:, at] = local_ref[:, at] + dot(left, right)
         if (tile + 1) % (all_tiles // STEPS) == 0:
@@ -285,8 +297,8 @@
             pltpu.VMEM((rows, width), BF16),
             pltpu.VMEM((shards * 17, LANES), F32),
             pltpu.VMEM((tiles, LANES, 2 * LANES), BF16),
-            pltpu.SemaphoreType.DMA((1 + 2 * STEPS,)),
-            pltpu.SemaphoreType.DMA((2 * STEPS,)),
+            pltpu.SemaphoreType.DMA((1 + 2 * HALVES,)),
+            pltpu.SemaphoreType.DMA((2 * HALVES,)),
         ],
         compiler_params=full,
         name="summary",
@@ -302,14 +314,19 @@
     decay = jnp.repeat(jnp.exp(-own_rates * rows), CG, axis=1)
 
     row = pl.BlockSpec((1, block), lambda q: (0, q))
-    local_in, weight = pl.pallas_call(
+    local_in, near, far = pl.pallas_call(
         local_kernel,
         grid=(STEPS,),
         in_specs=[whole((modes, groups)), row, row, slab],
-        out_specs=[slab, pl.BlockSpec((2 * rows, block), lambda q: (0, q))],
+        out_specs=[
+            slab,
+            pl.BlockSpec((SUB, block), lambda q: (0, q)),
+            pl.BlockSpec((rows // SUB, block), lambda q: (0, q)),
+        ],
         out_shape=[
             jax.ShapeDtypeStruct((rows, width), F32),
-            jax.ShapeDtypeStruct((2 * rows, width), BF16),
+            jax.ShapeDtypeStruct((SUB, width), F32),
+            jax.ShapeDtypeStruct((rows // SUB, width), F32),
         ],
         compiler_params=vmem,
         name="local",
@@ -339,7 +356,12 @@
         others.append(lax.ppermute(mine, ("seq_x", "seq_core"), pairs))
     grad_in = pl.pallas_call(
         carry_kernel,
-        in_specs=[whole((shards * 9, LANES)), whole((rows, width)), whole((2 * rows, width))],
+        in_specs=[
+            whole((shards * 9, LANES)),
+            whole((rows, width)),
+            whole((SUB, width)),
+            whole((rows // SUB, width)),
+        ],
         out_specs=anywhere,
         out_shape=jax.ShapeDtypeStruct((rows, width), F32),
         scratch_shapes=[pltpu.VMEM((rows, width), F32), pltpu.SemaphoreType.DMA((STEPS,))],
@@ -348,7 +370,7 @@
         cost_estimate=pl.CostEstimate(
             flops=8 * 10**8, bytes_accessed=7 * 2**20, transcendentals=0
         ),
-    )(back.reshape(shards * 9, LANES), local_in, weight)
+    )(back.reshape(shards * 9, LANES), local_in, near, far)
     grad_res = pl.pallas_call(
         finish_kernel,
         out_shape=jax.ShapeDtypeStruct((modes, groups), F32),

time: 70.5 us -> 68.6 us (0.973)
  local copies, waits for them, and re-layouts: 4.74 us -> 1.83 us
  waiting for transfers between devices: 6.28 us -> 7.96 us
    unnamed x10 -> x6, local copies, waits for them, and re-layouts: 4.13 us -> 1.23 us
    all_to_all x1, waiting for transfers between devices: 6.27 us -> 7.82 us  [local(): lax.all_to_all(sent.reshape(shards, 1, 17 * LANES), CTX, 0, 0, tiled=True)]
  transfers between devices with their start and end apart: 4 -> 4, of which waited for: 1 -> 2; matrix products, arithmetic and copies ran while one was open for 1% -> 1% of each run, Pallas kernels for 15% -> 15%
where the time goes in v3:
time: 68.6 us; the launch traced here: 68.3 us
  starting transfers between devices  20.5 us (30%)
  blocking collectives  19.1 us (28%)
  Pallas kernels  18.1 us (26%)
  waiting for transfers between devices  7.96 us (12%)
  local copies, waits for them, and re-layouts  1.83 us (3%)
  between operations  0.78 us (1%)
    all_to_all x1, blocking collectives, local(): lax.all_to_all(states.reshape(shards, 1, 9 * LANES), CTX, 0, 0, tiled=True)  19.1 us
    all_to_all x1, starting transfers between devices, local(): lax.all_to_all(sent.reshape(shards, 1, 17 * LANES), CTX, 0, 0, tiled=True)  15.1 us
    pallas_call x1, Pallas kernels, local(): pl.pallas_call(local_kernel, grid=(STEPS,), in_specs=[whole((modes, group...  8.39 us
    all_to_all x1, waiting for transfers between devices, local(): lax.all_to_all(sent.reshape(shards, 1, 17 * LANES), CTX, 0, 0, tiled=True)  7.82 us
    pallas_call x1, Pallas kernels, local(): pl.pallas_call(summary_kernel, in_specs=[anywhere, anywhere, anywhere], o...  6.6 us
    ppermute x3, starting transfers between devices, local(): others.append(lax.ppermute(mine, ('seq_x', 'seq_core'), pairs))  5.35 us
    pallas_call x1, Pallas kernels, local(): pl.pallas_call(carry_kernel, in_specs=[whole((shards * 9, LANES)), whole(...  1.81 us
  transfers between devices with their start and end apart: 4, of which 2 were waited for; matrix products, arithmetic and copies ran while one was open for 1% of the time, Pallas kernels for 15%

profile of v3, /device:TPU:1, one launch (start us, length us, event | category | flops | bytes accessed | tf_op | source)
XLA Modules:
  0.0 68.3 jit_solution(15299706470558619377)
XLA Ops:
  0.6 0.0 copy-start.1
  0.7 6.6 %summary.1 = f32[1088,128]{1,0:T(8,128)} custom-call(f32[16,256]{1,0:T(8,128)} %rates_ref.1, bf16[128,4096]{1,0:T(8,128)(2,1)} %bitcast.17, bf16[128,4096]{1,0:T(8,128)(2,1)} %bitcast.26), custom_call_target="tpu_custom_call" | custom-call | tf_op jit(solution)/shard_map/summary/pallas_call | solution.py:289
  7.3 15.1 %all-to-all-start = ((f32[64,1,2176]{2,1,0:T(1,128)}), f32[64,1,2176]{2,1,0:T(1,128)S(1)}, u32[]{:S(2)}, u32[]{:S(2)}) async-start(f32[64,1,2176]{2,1,0:T(1,128)} %bitcast.24), calls=%async_computation | async-start | bytes 1114112 | tf_op jit(solution)/shard_map/all_to_all | solution.py:306
  22.4 0.1 multiply_exponential_fusion
  22.5 0.1 broadcast_in_dim.10
  22.6 0.1 reshape.25.decay_ref
  22.7 0.1 copy.11
  22.8 0.1 reshape.28.amp_row_ref
  22.9 0.1 copy.10
  23.0 0.1 reshape.27.rate_row_ref
  23.1 0.0 copy-start
  23.2 1.2 %copy-done = bf16[1,128,4096]{2,1,0:T(8,128)(2,1)S(1)} copy-done((bf16[1,128,4096]{2,1,0:T(8,128)(2,1)S(1)}, bf16[1,128,4096]{2,1,0:T(8,128)(2,1)}, u32[]{:S(2)}) %copy-start) | copy-done | bytes 1048600
  24.4 8.4 %local.1 = (f32[128,4096]{1,0:T(8,128)S(1)}, f32[16,4096]{1,0:T(8,128)S(1)}, f32[8,4096]{1,0:T(8,128)S(1)}) custom-call(f32[16,256]{1,0:T(8,128)S(1)} %copy-done.1, f32[1,4096]{1,0:T(1,128)S(1)} %reshape.27.rate_row_ref, f32[1,4096]{1,0:T(1,128)S(1)} %reshape.28.amp_row_ref, bf16[128,4096]{1,0:T(8,128)(2,1)S(1)} %bitcast.18), custom_call_target="tpu_custom_call" | custom-call | flops 8000000000 | bytes 5242880 | tf_op jit(solution)/shard_map/local/pallas_call | solution.py:317
  32.8 7.8 %all-to-all-done = f32[64,1,2176]{2,1,0:T(1,128)S(1)} async-done(((f32[64,1,2176]{2,1,0:T(1,128)}), f32[64,1,2176]{2,1,0:T(1,128)S(1)}, u32[]{:S(2)}, u32[]{:S(2)}) %all-to-all-start) | async-done | bytes 557088 | tf_op jit(solution)/shard_map/all_to_all | solution.py:306
  40.6 0.3 scan.1
  40.9 19.1 %all_to_all.10 = f32[64,1,1152]{2,1,0:T(1,128)S(1)} all-to-all(f32[64,1,1152]{2,1,0:T(1,128)S(1)} %bitcast.16), channel_id=1, replica_groups=mesh['seq_x'=2,'seq_core'=2,'ctx_0'=2,'ctx_1'=8,'ctx_2'=4] {'ctx_0','ctx..., dimensions={0} | all-to-all | bytes 589824 | tf_op jit(solution)/shard_map/all_to_all | solution.py:350
  60.1 4.2 %collective-permute-start.2 = (f32[64,128]{1,0:T(8,128)S(1)}, f32[64,128]{1,0:T(8,128)S(1)}, u32[]{:S(2)}, u32[]{:S(2)}) collective-permute-start(f32[64,128]{1,0:T(8,128)S(1)} %bitcast.20), channel_id=1, source_target_pairs={{0,192},{64,128},{128,64},{192,0},{1,193},{65,129},{129,65},{193,1... | collective-permute-start | bytes 98312 | tf_op jit(solution)/shard_map/ppermute | solution.py:356
  64.2 1.2 %collective-permute-start.1 = (f32[64,128]{1,0:T(8,128)S(1)}, f32[64,128]{1,0:T(8,128)S(1)}, u32[]{:S(2)}, u32[]{:S(2)}) collective-permute-start(f32[64,128]{1,0:T(8,128)S(1)} %bitcast.21), channel_id=1, source_target_pairs={{0,128},{64,192},{128,0},{192,64},{1,129},{65,193},{129,1},{193,65... | collective-permute-start | bytes 98312 | tf_op jit(solution)/shard_map/ppermute | solution.py:356
  65.4 0.0 collective-permute-start
  65.4 1.8 %carry.1 = f32[128,4096]{1,0:T(8,128)} custom-call(f32[576,128]{1,0:T(8,128)S(1)} %bitcast.15, f32[128,4096]{1,0:T(8,128)S(1)} %get-tuple-element.9.local_ref, f32[16,4096]{1,0:T(8,128)S(1)} %get-tuple-element.10.near_ref, f32[8,4096]{1,0:T(8,128)S(1)} %get-tuple-element.11.far_ref), custom_call_target="tpu_custom_call" | custom-call | flops 800000000 | bytes 7340032 | tf_op jit(solution)/shard_map/carry/pallas_call | solution.py:357
  67.2 0.0 collective-permute-done.2.d_ref
  67.2 0.1 collective-permute-done.1.c_ref
  67.4 0.0 collective-permute-done.b_ref
  67.4 0.9 %finish.1 = f32[16,256]{1,0:T(8,128)} custom-call(f32[16,256]{1,0:T(8,128)S(1)} %get-tuple-element.12.factor_ref, f32[64,128]{1,0:T(8,128)S(1)} %bitcast.23, f32[64,128]{1,0:T(8,128)S(1)} %collective-permute-done.b_ref, f32[64,128]{1,0:T(8,128)S(1)} %collective-permute-done.1.c_ref, f32[64,128]{1,0:T(8,128)S(1)} %collective-permute-done.2.d_ref), custom_call_target="tpu_custom_call" | custom-call | tf_op jit(solution)/shard_map/finish/pallas_call | solution.py:374
  (5 shorter events, 0.1 us)
Async XLA Ops:
  0.6 21.8 %copy-start.1 = (f32[16,256]{1,0:T(8,128)S(1)}, f32[16,256]{1,0:T(8,128)}, u32[]{:S(2)}) copy-start(f32[16,256]{1,0:T(8,128)} %rates_ref.1) | copy-start | bytes 49156
  0.6 22.0 %copy-start.2 = (f32[16,256]{1,0:T(8,128)S(1)}, f32[16,256]{1,0:T(8,128)}, u32[]{:S(2)}) copy-start(f32[16,256]{1,0:T(8,128)} %param.6) | copy-start | bytes 49156
  7.3 33.3 %all-to-all-start = ((f32[64,1,2176]{2,1,0:T(1,128)}), f32[64,1,2176]{2,1,0:T(1,128)S(1)}, u32[]{:S(2)}, u32[]{:S(2)}) async-start(f32[64,1,2176]{2,1,0:T(1,128)} %bitcast.24), calls=%async_computation | async-start | bytes 1114112 | tf_op jit(solution)/shard_map/all_to_all | solution.py:306
  23.1 1.2 %copy-start = (bf16[1,128,4096]{2,1,0:T(8,128)(2,1)S(1)}, bf16[1,128,4096]{2,1,0:T(8,128)(2,1)}, u32[]{:S(2)}) copy-start(bf16[1,128,4096]{2,1,0:T(8,128)(2,1)} %param.4) | copy-start | bytes 3145732
  60.1 7.2 %collective-permute-start.2 = (f32[64,128]{1,0:T(8,128)S(1)}, f32[64,128]{1,0:T(8,128)S(1)}, u32[]{:S(2)}, u32[]{:S(2)}) collective-permute-start(f32[64,128]{1,0:T(8,128)S(1)} %bitcast.20), channel_id=1, source_target_pairs={{0,192},{64,128},{128,64},{192,0},{1,193},{65,129},{129,65},{193,1... | collective-permute-start | bytes 98312 | tf_op jit(solution)/shard_map/ppermute | solution.py:356
  64.2 3.1 %collective-permute-start.1 = (f32[64,128]{1,0:T(8,128)S(1)}, f32[64,128]{1,0:T(8,128)S(1)}, u32[]{:S(2)}, u32[]{:S(2)}) collective-permute-start(f32[64,128]{1,0:T(8,128)S(1)} %bitcast.21), channel_id=1, source_target_pairs={{0,128},{64,192},{128,0},{192,64},{1,129},{65,193},{129,1},{193,65... | collective-permute-start | bytes 98312 | tf_op jit(solution)/shard_map/ppermute | solution.py:356
  65.4 2.0 %collective-permute-start = (f32[64,128]{1,0:T(8,128)S(1)}, f32[64,128]{1,0:T(8,128)S(1)}, u32[]{:S(2)}, u32[]{:S(2)}) collective-permute-start(f32[64,128]{1,0:T(8,128)S(1)} %bitcast.22), channel_id=1, source_target_pairs={{0,64},{64,0},{128,192},{192,128},{1,65},{65,1},{129,193},{193,129... | collective-permute-start | bytes 98312 | tf_op jit(solution)/shard_map/ppermute | solution.py:356

commit v4 on v3

--- a/solution.py
+++ b/solution.py
@@ -15,7 +15,6 @@
 HALVES = 2
 F32 = jnp.float32
 BF16 = jnp.bfloat16
-HIGHEST = lax.Precision.HIGHEST
 
 
 def iota(shape, dim):
@@ -209,14 +208,8 @@
         total = total + in_ref[17 * j + 8 : 17 * j + 16, :] * state
         row = row + in_ref[17 * j + 16 : 17 * j + 17, :]
         state = in_ref[17 * j : 17 * j + 8, :] + decay * state
-    same = iota((LANES, LANES), 0) // CG == iota((LANES, LANES), 1) // CG
-    summed = lax.dot_general(
-        total,
-        same.astype(F32),
-        (((1,), (0,)), ((), ())),
-        precision=HIGHEST,
-        preferred_element_type=F32,
-    )
+    same = iota((2 * LANES, LANES), 0) // CG % GT == iota((2 * LANES, LANES), 1) // CG
+    summed = dot(jnp.concatenate(split(total), 1), same.astype(F32).astype(BF16))
     place = iota((8, LANES), 1) % CG == iota((8, LANES), 0) + half_ref[0]
     row = row + jnp.sum(jnp.where(place, summed, 0.0), axis=0, keepdims=True)
     for j in range(shards):
@@ -259,10 +252,10 @@
     modes, groups = out_ref.shape
     early = iota((count, LANES), 1) % CG < modes // 2
     total = jnp.where(early, total[:count], total[count:])
-    pick = (iota((count, groups), 0) == iota((count, groups), 1) // GT).astype(F32)
+    pick = iota((2 * count, groups), 0) % count == iota((2 * count, groups), 1) // GT
     keep = iota((GT, CG, groups), 0) == iota((GT, CG, groups), 2) % GT
-    spread = lax.dot_general(
-        total, pick, (((0,), (0,)), ((), ())), precision=HIGHEST, preferred_element_type=F32
+    spread = dot(
+        jnp.concatenate(split(total), 0), pick.astype(F32).astype(BF16), ((0,), (0,))
     ).reshape(GT, CG, groups)
     out_ref[...] = jnp.sum(jnp.where(keep, spread, 0.0), axis=0) * factor_ref[...]
 

time: 68.6 us -> 68.4 us (level)
  no operation moved by 1% of the time
where the time goes in v4:
time: 68.4 us; the launch traced here: 68.2 us
  starting transfers between devices  20.5 us (30%)
  blocking collectives  19.1 us (28%)
  Pallas kernels  17.9 us (26%)
  waiting for transfers between devices  7.96 us (12%)
  local copies, waits for them, and re-layouts  1.83 us (3%)
  between operations  0.78 us (1%)
    all_to_all x1, blocking collectives, local(): lax.all_to_all(states.reshape(shards, 1, 9 * LANES), CTX, 0, 0, tiled=True)  19.1 us
    all_to_all x1, starting transfers between devices, local(): lax.all_to_all(sent.reshape(shards, 1, 17 * LANES), CTX, 0, 0, tiled=True)  15.1 us
    pallas_call x1, Pallas kernels, local(): pl.pallas_call(local_kernel, grid=(STEPS,), in_specs=[whole((modes, group...  8.39 us
    all_to_all x1, waiting for transfers between devices, local(): lax.all_to_all(sent.reshape(shards, 1, 17 * LANES), CTX, 0, 0, tiled=True)  7.82 us
    pallas_call x1, Pallas kernels, local(): pl.pallas_call(summary_kernel, in_specs=[anywhere, anywhere, anywhere], o...  6.6 us
    ppermute x3, starting transfers between devices, local(): others.append(lax.ppermute(mine, ('seq_x', 'seq_core'), pairs))  5.35 us
    pallas_call x1, Pallas kernels, local(): pl.pallas_call(carry_kernel, in_specs=[whole((shards * 9, LANES)), whole(...  1.82 us
  transfers between devices with their start and end apart: 4, of which 2 were waited for; matrix products, arithmetic and copies ran while one was open for 1% of the time, Pallas kernels for 15%

profile of v4, /device:TPU:1, one launch (start us, length us, event | category | flops | bytes accessed | tf_op | source)
XLA Modules:
  0.0 68.2 jit_solution(1519164804816153282)
XLA Ops:
  0.6 0.0 copy-start.1
  0.7 6.6 %summary.1 = f32[1088,128]{1,0:T(8,128)} custom-call(f32[16,256]{1,0:T(8,128)} %rates_ref.1, bf16[128,4096]{1,0:T(8,128)(2,1)} %bitcast.17, bf16[128,4096]{1,0:T(8,128)(2,1)} %bitcast.26), custom_call_target="tpu_custom_call" | custom-call | tf_op jit(solution)/shard_map/summary/pallas_call | solution.py:282
  7.3 15.1 %all-to-all-start = ((f32[64,1,2176]{2,1,0:T(1,128)}), f32[64,1,2176]{2,1,0:T(1,128)S(1)}, u32[]{:S(2)}, u32[]{:S(2)}) async-start(f32[64,1,2176]{2,1,0:T(1,128)} %bitcast.24), calls=%async_computation | async-start | bytes 1114112 | tf_op jit(solution)/shard_map/all_to_all | solution.py:299
  22.4 0.1 multiply_exponential_fusion
  22.5 0.1 broadcast_in_dim.10
  22.6 0.1 reshape.25.decay_ref
  22.7 0.1 copy.11
  22.8 0.1 reshape.28.amp_row_ref
  22.9 0.1 copy.10
  23.0 0.1 reshape.27.rate_row_ref
  23.1 0.0 copy-start
  23.2 1.2 %copy-done = bf16[1,128,4096]{2,1,0:T(8,128)(2,1)S(1)} copy-done((bf16[1,128,4096]{2,1,0:T(8,128)(2,1)S(1)}, bf16[1,128,4096]{2,1,0:T(8,128)(2,1)}, u32[]{:S(2)}) %copy-start) | copy-done | bytes 1048600
  24.4 8.4 %local.1 = (f32[128,4096]{1,0:T(8,128)S(1)}, f32[16,4096]{1,0:T(8,128)S(1)}, f32[8,4096]{1,0:T(8,128)S(1)}) custom-call(f32[16,256]{1,0:T(8,128)S(1)} %copy-done.1, f32[1,4096]{1,0:T(1,128)S(1)} %reshape.27.rate_row_ref, f32[1,4096]{1,0:T(1,128)S(1)} %reshape.28.amp_row_ref, bf16[128,4096]{1,0:T(8,128)(2,1)S(1)} %bitcast.18), custom_call_target="tpu_custom_call" | custom-call | flops 8000000000 | bytes 5242880 | tf_op jit(solution)/shard_map/local/pallas_call | solution.py:310
  32.8 7.8 %all-to-all-done = f32[64,1,2176]{2,1,0:T(1,128)S(1)} async-done(((f32[64,1,2176]{2,1,0:T(1,128)}), f32[64,1,2176]{2,1,0:T(1,128)S(1)}, u32[]{:S(2)}, u32[]{:S(2)}) %all-to-all-start) | async-done | bytes 557088 | tf_op jit(solution)/shard_map/all_to_all | solution.py:299
  40.6 0.3 scan.1
  40.9 19.1 %all_to_all.10 = f32[64,1,1152]{2,1,0:T(1,128)S(1)} all-to-all(f32[64,1,1152]{2,1,0:T(1,128)S(1)} %bitcast.16), channel_id=1, replica_groups=mesh['seq_x'=2,'seq_core'=2,'ctx_0'=2,'ctx_1'=8,'ctx_2'=4] {'ctx_0','ctx..., dimensions={0} | all-to-all | bytes 589824 | tf_op jit(solution)/shard_map/all_to_all | solution.py:343
  60.0 4.2 %collective-permute-start.2 = (f32[64,128]{1,0:T(8,128)S(1)}, f32[64,128]{1,0:T(8,128)S(1)}, u32[]{:S(2)}, u32[]{:S(2)}) collective-permute-start(f32[64,128]{1,0:T(8,128)S(1)} %bitcast.20), channel_id=1, source_target_pairs={{0,192},{64,128},{128,64},{192,0},{1,193},{65,129},{129,65},{193,1... | collective-permute-start | bytes 98312 | tf_op jit(solution)/shard_map/ppermute | solution.py:349
  64.2 1.2 %collective-permute-start.1 = (f32[64,128]{1,0:T(8,128)S(1)}, f32[64,128]{1,0:T(8,128)S(1)}, u32[]{:S(2)}, u32[]{:S(2)}) collective-permute-start(f32[64,128]{1,0:T(8,128)S(1)} %bitcast.21), channel_id=1, source_target_pairs={{0,128},{64,192},{128,0},{192,64},{1,129},{65,193},{129,1},{193,65... | collective-permute-start | bytes 98312 | tf_op jit(solution)/shard_map/ppermute | solution.py:349
  65.4 0.0 collective-permute-start
  65.4 1.8 %carry.1 = f32[128,4096]{1,0:T(8,128)} custom-call(f32[576,128]{1,0:T(8,128)S(1)} %bitcast.15, f32[128,4096]{1,0:T(8,128)S(1)} %get-tuple-element.9.local_ref, f32[16,4096]{1,0:T(8,128)S(1)} %get-tuple-element.10.near_ref, f32[8,4096]{1,0:T(8,128)S(1)} %get-tuple-element.11.far_ref), custom_call_target="tpu_custom_call" | custom-call | flops 800000000 | bytes 7340032 | tf_op jit(solution)/shard_map/carry/pallas_call | solution.py:350
  67.2 0.0 collective-permute-done.2.d_ref
  67.2 0.1 collective-permute-done.1.c_ref
  67.4 0.0 collective-permute-done.b_ref
  67.4 0.8 %finish.1 = f32[16,256]{1,0:T(8,128)} custom-call(f32[16,256]{1,0:T(8,128)S(1)} %get-tuple-element.12.factor_ref, f32[64,128]{1,0:T(8,128)S(1)} %bitcast.23, f32[64,128]{1,0:T(8,128)S(1)} %collective-permute-done.b_ref, f32[64,128]{1,0:T(8,128)S(1)} %collective-permute-done.1.c_ref, f32[64,128]{1,0:T(8,128)S(1)} %collective-permute-done.2.d_ref), custom_call_target="tpu_custom_call" | custom-call | tf_op jit(solution)/shard_map/finish/pallas_call | solution.py:367
  (5 shorter events, 0.1 us)
Async XLA Ops:
  0.6 21.8 %copy-start.1 = (f32[16,256]{1,0:T(8,128)S(1)}, f32[16,256]{1,0:T(8,128)}, u32[]{:S(2)}) copy-start(f32[16,256]{1,0:T(8,128)} %rates_ref.1) | copy-start | bytes 49156
  0.6 22.0 %copy-start.2 = (f32[16,256]{1,0:T(8,128)S(1)}, f32[16,256]{1,0:T(8,128)}, u32[]{:S(2)}) copy-start(f32[16,256]{1,0:T(8,128)} %param.6) | copy-start | bytes 49156
  7.3 33.3 %all-to-all-start = ((f32[64,1,2176]{2,1,0:T(1,128)}), f32[64,1,2176]{2,1,0:T(1,128)S(1)}, u32[]{:S(2)}, u32[]{:S(2)}) async-start(f32[64,1,2176]{2,1,0:T(1,128)} %bitcast.24), calls=%async_computation | async-start | bytes 1114112 | tf_op jit(solution)/shard_map/all_to_all | solution.py:299
  23.1 1.2 %copy-start = (bf16[1,128,4096]{2,1,0:T(8,128)(2,1)S(1)}, bf16[1,128,4096]{2,1,0:T(8,128)(2,1)}, u32[]{:S(2)}) copy-start(bf16[1,128,4096]{2,1,0:T(8,128)(2,1)} %param.4) | copy-start | bytes 3145732
  60.0 7.2 %collective-permute-start.2 = (f32[64,128]{1,0:T(8,128)S(1)}, f32[64,128]{1,0:T(8,128)S(1)}, u32[]{:S(2)}, u32[]{:S(2)}) collective-permute-start(f32[64,128]{1,0:T(8,128)S(1)} %bitcast.20), channel_id=1, source_target_pairs={{0,192},{64,128},{128,64},{192,0},{1,193},{65,129},{129,65},{193,1... | collective-permute-start | bytes 98312 | tf_op jit(solution)/shard_map/ppermute | solution.py:349
  64.2 3.1 %collective-permute-start.1 = (f32[64,128]{1,0:T(8,128)S(1)}, f32[64,128]{1,0:T(8,128)S(1)}, u32[]{:S(2)}, u32[]{:S(2)}) collective-permute-start(f32[64,128]{1,0:T(8,128)S(1)} %bitcast.21), channel_id=1, source_target_pairs={{0,128},{64,192},{128,0},{192,64},{1,129},{65,193},{129,1},{193,65... | collective-permute-start | bytes 98312 | tf_op jit(solution)/shard_map/ppermute | solution.py:349
  65.4 2.0 %collective-permute-start = (f32[64,128]{1,0:T(8,128)S(1)}, f32[64,128]{1,0:T(8,128)S(1)}, u32[]{:S(2)}, u32[]{:S(2)}) collective-permute-start(f32[64,128]{1,0:T(8,128)S(1)} %bitcast.22), channel_id=1, source_target_pairs={{0,64},{64,0},{128,192},{192,128},{1,65},{65,1},{129,193},{193,129... | collective-permute-start | bytes 98312 | tf_op jit(solution)/shard_map/ppermute | solution.py:349

commit v5 on v4

--- a/solution.py
+++ b/solution.py
@@ -13,6 +13,7 @@
 SUB = 16
 STEPS = 4
 HALVES = 2
+PIECES = 8
 F32 = jnp.float32
 BF16 = jnp.bfloat16
 
@@ -212,6 +213,8 @@
     summed = dot(jnp.concatenate(split(total), 1), same.astype(F32).astype(BF16))
     place = iota((8, LANES), 1) % CG == iota((8, LANES), 0) + half_ref[0]
     row = row + jnp.sum(jnp.where(place, summed, 0.0), axis=0, keepdims=True)
+    own = iota((1, LANES), 1) % CG - half_ref[0]
+    row = jnp.where((own >= 0) & (own < 8), row, 0.0)
     for j in range(shards):
         out_ref[9 * j + 8 : 9 * j + 9, :] = row
 
@@ -219,7 +222,7 @@
 def carry_kernel(state_ref, local_ref, near_ref, far_ref, out_hbm, out_ref, sems):
     rows, width = out_ref.shape
     all_tiles = width // LANES
-    block = width // STEPS
+    block = width // PIECES
     stores = []
     for tile in range(all_tiles):
         at = pl.ds(tile * LANES, LANES)
@@ -235,8 +238,8 @@
         left = jnp.concatenate([high, low, high], 1)
         right = jnp.concatenate([rights[0], rights[0], rights[1]], 0)
         out_ref[:, at] = local_ref[:, at] + dot(left, right)
-        if (tile + 1) % (all_tiles // STEPS) == 0:
-            q = tile // (all_tiles // STEPS)
+        if (tile + 1) % (all_tiles // PIECES) == 0:
+            q = tile // (all_tiles // PIECES)
             at = pl.ds(q * block, block)
             stores.append(
                 pltpu.make_async_copy(out_ref.at[:, at], out_hbm.at[:, at], sems.at[q])
@@ -248,10 +251,8 @@
 
 def finish_kernel(factor_ref, a_ref, b_ref, c_ref, d_ref, out_ref):
     total = (a_ref[...] + b_ref[...]) + (c_ref[...] + d_ref[...])
-    count = total.shape[0] // 2
-    modes, groups = out_ref.shape
-    early = iota((count, LANES), 1) % CG < modes // 2
-    total = jnp.where(early, total[:count], total[count:])
+    count = total.shape[0]
+    groups = out_ref.shape[1]
     pick = iota((2 * count, groups), 0) % count == iota((2 * count, groups), 1) // GT
     keep = iota((GT, CG, groups), 0) == iota((GT, CG, groups), 2) % GT
     spread = dot(
@@ -342,7 +343,8 @@
     )(first_mode[None], decay, got.reshape(shards * 17, LANES))
     back = lax.all_to_all(states.reshape(shards, 1, 9 * LANES), CTX, 0, 0, tiled=True)
 
-    mine = back[:, 0, 8 * LANES :]
+    sums = back[:, 0, 8 * LANES :]
+    mine = sums[:tiles] + sums[tiles:]
     others = [mine]
     for bits in (1, 2, 3):
         pairs = [(d, d ^ bits) for d in range(4)]
@@ -357,7 +359,7 @@
         ],
         out_specs=anywhere,
         out_shape=jax.ShapeDtypeStruct((rows, width), F32),
-        scratch_shapes=[pltpu.VMEM((rows, width), F32), pltpu.SemaphoreType.DMA((STEPS,))],
+        scratch_shapes=[pltpu.VMEM((rows, width), F32), pltpu.SemaphoreType.DMA((PIECES,))],
         compiler_params=vmem,
         name="carry",
         cost_estimate=pl.CostEstimate(

time: 68.4 us -> 68.3 us (level)
  transfers between devices with their start and end apart: 4 -> 4, of which waited for: 2 -> 1; matrix products, arithmetic and copies ran while one was open for 1% -> 1% of each run, Pallas kernels for 15% -> 15%
where the time goes in v5:
time: 68.3 us; the launch traced here: 68 us
  starting transfers between devices  20.5 us (30%)
  blocking collectives  19.1 us (28%)
  Pallas kernels  17.9 us (26%)
  waiting for transfers between devices  7.83 us (11%)
  local copies, waits for them, and re-layouts  1.83 us (3%)
  between operations  0.8 us (1%)
    all_to_all x1, blocking collectives, local(): lax.all_to_all(states.reshape(shards, 1, 9 * LANES), CTX, 0, 0, tiled=True)  19.1 us
    all_to_all x1, starting transfers between devices, local(): lax.all_to_all(sent.reshape(shards, 1, 17 * LANES), CTX, 0, 0, tiled=True)  15.1 us
    pallas_call x1, Pallas kernels, local(): pl.pallas_call(local_kernel, grid=(STEPS,), in_specs=[whole((modes, group...  8.39 us
    all_to_all x1, waiting for transfers between devices, local(): lax.all_to_all(sent.reshape(shards, 1, 17 * LANES), CTX, 0, 0, tiled=True)  7.82 us
    pallas_call x1, Pallas kernels, local(): pl.pallas_call(summary_kernel, in_specs=[anywhere, anywhere, anywhere], o...  6.6 us
    ppermute x3, starting transfers between devices, local(): others.append(lax.ppermute(mine, ('seq_x', 'seq_core'), pairs))  5.35 us
    pallas_call x1, Pallas kernels, local(): pl.pallas_call(carry_kernel, in_specs=[whole((shards * 9, LANES)), whole(...  1.76 us
  transfers between devices with their start and end apart: 4, of which 1 were waited for; matrix products, arithmetic and copies ran while one was open for 1% of the time, Pallas kernels for 15%

profile of v5, /device:TPU:1, one launch (start us, length us, event | category | flops | bytes accessed | tf_op | source)
XLA Modules:
  0.0 68.0 jit_solution(11622894526836636209)
XLA Ops:
  0.6 0.0 copy-start.1
  0.7 6.6 %summary.1 = f32[1088,128]{1,0:T(8,128)} custom-call(f32[16,256]{1,0:T(8,128)} %rates_ref.1, bf16[128,4096]{1,0:T(8,128)(2,1)} %bitcast.18, bf16[128,4096]{1,0:T(8,128)(2,1)} %bitcast.23), custom_call_target="tpu_custom_call" | custom-call | tf_op jit(solution)/shard_map/summary/pallas_call | solution.py:283
  7.3 15.1 %all-to-all-start = ((f32[64,1,2176]{2,1,0:T(1,128)}), f32[64,1,2176]{2,1,0:T(1,128)S(1)}, u32[]{:S(2)}, u32[]{:S(2)}) async-start(f32[64,1,2176]{2,1,0:T(1,128)} %bitcast.21), calls=%async_computation | async-start | bytes 1114112 | tf_op jit(solution)/shard_map/all_to_all | solution.py:300
  22.4 0.1 multiply_exponential_fusion
  22.5 0.1 broadcast_in_dim.10
  22.6 0.1 reshape.28.decay_ref
  22.7 0.1 copy.11
  22.8 0.1 reshape.31.amp_row_ref
  22.9 0.1 copy.10
  23.0 0.1 reshape.30.rate_row_ref
  23.1 0.0 copy-start
  23.2 1.2 %copy-done = bf16[1,128,4096]{2,1,0:T(8,128)(2,1)S(1)} copy-done((bf16[1,128,4096]{2,1,0:T(8,128)(2,1)S(1)}, bf16[1,128,4096]{2,1,0:T(8,128)(2,1)}, u32[]{:S(2)}) %copy-start) | copy-done | bytes 1048600
  24.4 8.4 %local.1 = (f32[128,4096]{1,0:T(8,128)S(1)}, f32[16,4096]{1,0:T(8,128)S(1)}, f32[8,4096]{1,0:T(8,128)S(1)}) custom-call(f32[16,256]{1,0:T(8,128)S(1)} %copy-done.1, f32[1,4096]{1,0:T(1,128)S(1)} %reshape.30.rate_row_ref, f32[1,4096]{1,0:T(1,128)S(1)} %reshape.31.amp_row_ref, bf16[128,4096]{1,0:T(8,128)(2,1)S(1)} %bitcast.19), custom_call_target="tpu_custom_call" | custom-call | flops 8000000000 | bytes 5242880 | tf_op jit(solution)/shard_map/local/pallas_call | solution.py:311
  32.8 7.8 %all-to-all-done = f32[64,1,2176]{2,1,0:T(1,128)S(1)} async-done(((f32[64,1,2176]{2,1,0:T(1,128)}), f32[64,1,2176]{2,1,0:T(1,128)S(1)}, u32[]{:S(2)}, u32[]{:S(2)}) %all-to-all-start) | async-done | bytes 557088 | tf_op jit(solution)/shard_map/all_to_all | solution.py:300
  40.6 0.3 scan.1
  40.9 19.1 %all_to_all.10 = f32[64,1,1152]{2,1,0:T(1,128)S(1)} all-to-all(f32[64,1,1152]{2,1,0:T(1,128)S(1)} %bitcast.17), channel_id=1, replica_groups=mesh['seq_x'=2,'seq_core'=2,'ctx_0'=2,'ctx_1'=8,'ctx_2'=4] {'ctx_0','ctx..., dimensions={0} | all-to-all | bytes 589824 | tf_op jit(solution)/shard_map/all_to_all | solution.py:344
  60.1 4.2 %collective-permute-start.2 = (f32[32,128]{1,0:T(8,128)S(1)}, f32[32,128]{1,0:T(8,128)S(1)}, u32[]{:S(2)}, u32[]{:S(2)}) collective-permute-start(f32[32,128]{1,0:T(8,128)S(1)} %add_bitcast_fusion.a_ref), channel_id=1, source_target_pairs={{0,192},{64,128},{128,64},{192,0},{1,193},{65,129},{129,65},{193,1... | collective-permute-start | bytes 49160 | tf_op jit(solution)/shard_map/ppermute | solution.py:351
  64.2 1.2 %collective-permute-start.1 = (f32[32,128]{1,0:T(8,128)S(1)}, f32[32,128]{1,0:T(8,128)S(1)}, u32[]{:S(2)}, u32[]{:S(2)}) collective-permute-start(f32[32,128]{1,0:T(8,128)S(1)} %add_bitcast_fusion.a_ref), channel_id=1, source_target_pairs={{0,128},{64,192},{128,0},{192,64},{1,129},{65,193},{129,1},{193,65... | collective-permute-start | bytes 49160 | tf_op jit(solution)/shard_map/ppermute | solution.py:351
  65.4 0.0 collective-permute-start
  65.4 1.8 %carry.1 = f32[128,4096]{1,0:T(8,128)} custom-call(f32[576,128]{1,0:T(8,128)S(1)} %bitcast.16, f32[128,4096]{1,0:T(8,128)S(1)} %get-tuple-element.9.local_ref, f32[16,4096]{1,0:T(8,128)S(1)} %get-tuple-element.10.near_ref, f32[8,4096]{1,0:T(8,128)S(1)} %get-tuple-element.11.far_ref), custom_call_target="tpu_custom_call" | custom-call | flops 800000000 | bytes 7340032 | tf_op jit(solution)/shard_map/carry/pallas_call | solution.py:352
  67.2 0.0 collective-permute-done.2.d_ref
  67.2 0.0 collective-permute-done.1.c_ref
  67.2 0.0 collective-permute-done.b_ref
  67.2 0.8 %finish.1 = f32[16,256]{1,0:T(8,128)} custom-call(f32[16,256]{1,0:T(8,128)S(1)} %get-tuple-element.14.factor_ref, f32[32,128]{1,0:T(8,128)S(1)} %add_bitcast_fusion.a_ref, f32[32,128]{1,0:T(8,128)S(1)} %collective-permute-done.b_ref, f32[32,128]{1,0:T(8,128)S(1)} %collective-permute-done.1.c_ref, f32[32,128]{1,0:T(8,128)S(1)} %collective-permute-done.2.d_ref), custom_call_target="tpu_custom_call" | custom-call | tf_op jit(solution)/shard_map/finish/pallas_call | solution.py:369
  (6 shorter events, 0.1 us)
Async XLA Ops:
  0.6 21.8 %copy-start.1 = (f32[16,256]{1,0:T(8,128)S(1)}, f32[16,256]{1,0:T(8,128)}, u32[]{:S(2)}) copy-start(f32[16,256]{1,0:T(8,128)} %rates_ref.1) | copy-start | bytes 49156
  0.6 22.0 %copy-start.2 = (f32[16,256]{1,0:T(8,128)S(1)}, f32[16,256]{1,0:T(8,128)}, u32[]{:S(2)}) copy-start(f32[16,256]{1,0:T(8,128)} %param.6) | copy-start | bytes 49156
  7.3 33.3 %all-to-all-start = ((f32[64,1,2176]{2,1,0:T(1,128)}), f32[64,1,2176]{2,1,0:T(1,128)S(1)}, u32[]{:S(2)}, u32[]{:S(2)}) async-start(f32[64,1,2176]{2,1,0:T(1,128)} %bitcast.21), calls=%async_computation | async-start | bytes 1114112 | tf_op jit(solution)/shard_map/all_to_all | solution.py:300
  23.1 1.2 %copy-start = (bf16[1,128,4096]{2,1,0:T(8,128)(2,1)S(1)}, bf16[1,128,4096]{2,1,0:T(8,128)(2,1)}, u32[]{:S(2)}) copy-start(bf16[1,128,4096]{2,1,0:T(8,128)(2,1)} %param.4) | copy-start | bytes 3145732
  60.1 7.1 %collective-permute-start.2 = (f32[32,128]{1,0:T(8,128)S(1)}, f32[32,128]{1,0:T(8,128)S(1)}, u32[]{:S(2)}, u32[]{:S(2)}) collective-permute-start(f32[32,128]{1,0:T(8,128)S(1)} %add_bitcast_fusion.a_ref), channel_id=1, source_target_pairs={{0,192},{64,128},{128,64},{192,0},{1,193},{65,129},{129,65},{193,1... | collective-permute-start | bytes 49160 | tf_op jit(solution)/shard_map/ppermute | solution.py:351
  64.2 2.9 %collective-permute-start.1 = (f32[32,128]{1,0:T(8,128)S(1)}, f32[32,128]{1,0:T(8,128)S(1)}, u32[]{:S(2)}, u32[]{:S(2)}) collective-permute-start(f32[32,128]{1,0:T(8,128)S(1)} %add_bitcast_fusion.a_ref), channel_id=1, source_target_pairs={{0,128},{64,192},{128,0},{192,64},{1,129},{65,193},{129,1},{193,65... | collective-permute-start | bytes 49160 | tf_op jit(solution)/shard_map/ppermute | solution.py:351
  65.4 1.8 %collective-permute-start = (f32[32,128]{1,0:T(8,128)S(1)}, f32[32,128]{1,0:T(8,128)S(1)}, u32[]{:S(2)}, u32[]{:S(2)}) collective-permute-start(f32[32,128]{1,0:T(8,128)S(1)} %add_bitcast_fusion.a_ref), channel_id=1, source_target_pairs={{0,64},{64,0},{128,192},{192,128},{1,65},{65,1},{129,193},{193,129... | collective-permute-start | bytes 49160 | tf_op jit(solution)/shard_map/ppermute | solution.py:351

commit v6 on v5

--- a/solution.py
+++ b/solution.py
@@ -13,7 +13,7 @@
 SUB = 16
 STEPS = 4
 HALVES = 2
-PIECES = 8
+PIECES = 16
 F32 = jnp.float32
 BF16 = jnp.bfloat16
 

time: 68.3 us -> 68.3 us (level)
  no operation moved by 1% of the time
where the time goes in v6:
time: 68.3 us; the launch traced here: 68 us
  starting transfers between devices  20.5 us (30%)
  blocking collectives  19.1 us (28%)
  Pallas kernels  17.9 us (26%)
  waiting for transfers between devices  7.83 us (11%)
  local copies, waits for them, and re-layouts  1.83 us (3%)
  between operations  0.8 us (1%)
    all_to_all x1, blocking collectives, local(): lax.all_to_all(states.reshape(shards, 1, 9 * LANES), CTX, 0, 0, tiled=True)  19.1 us
    all_to_all x1, starting transfers between devices, local(): lax.all_to_all(sent.reshape(shards, 1, 17 * LANES), CTX, 0, 0, tiled=True)  15.1 us
    pallas_call x1, Pallas kernels, local(): pl.pallas_call(local_kernel, grid=(STEPS,), in_specs=[whole((modes, group...  8.39 us
    all_to_all x1, waiting for transfers between devices, local(): lax.all_to_all(sent.reshape(shards, 1, 17 * LANES), CTX, 0, 0, tiled=True)  7.82 us
    pallas_call x1, Pallas kernels, local(): pl.pallas_call(summary_kernel, in_specs=[anywhere, anywhere, anywhere], o...  6.6 us
    ppermute x3, starting transfers between devices, local(): others.append(lax.ppermute(mine, ('seq_x', 'seq_core'), pairs))  5.35 us
    pallas_call x1, Pallas kernels, local(): pl.pallas_call(carry_kernel, in_specs=[whole((shards * 9, LANES)), whole(...  1.78 us
  transfers between devices with their start and end apart: 4, of which 1 were waited for; matrix products, arithmetic and copies ran while one was open for 1% of the time, Pallas kernels for 15%

profile of v6, /device:TPU:1, one launch (start us, length us, event | category | flops | bytes accessed | tf_op | source)
XLA Modules:
  0.0 68.0 jit_solution(8062811741770653568)
XLA Ops:
  0.6 0.0 copy-start.1
  0.7 6.6 %summary.1 = f32[1088,128]{1,0:T(8,128)} custom-call(f32[16,256]{1,0:T(8,128)} %rates_ref.1, bf16[128,4096]{1,0:T(8,128)(2,1)} %bitcast.18, bf16[128,4096]{1,0:T(8,128)(2,1)} %bitcast.23), custom_call_target="tpu_custom_call" | custom-call | tf_op jit(solution)/shard_map/summary/pallas_call | solution.py:283
  7.3 15.1 %all-to-all-start = ((f32[64,1,2176]{2,1,0:T(1,128)}), f32[64,1,2176]{2,1,0:T(1,128)S(1)}, u32[]{:S(2)}, u32[]{:S(2)}) async-start(f32[64,1,2176]{2,1,0:T(1,128)} %bitcast.21), calls=%async_computation | async-start | bytes 1114112 | tf_op jit(solution)/shard_map/all_to_all | solution.py:300
  22.4 0.1 multiply_exponential_fusion
  22.5 0.1 broadcast_in_dim.10
  22.6 0.1 reshape.28.decay_ref
  22.7 0.1 copy.11
  22.8 0.1 reshape.31.amp_row_ref
  22.9 0.1 copy.10
  23.0 0.1 reshape.30.rate_row_ref
  23.1 0.0 copy-start
  23.2 1.2 %copy-done = bf16[1,128,4096]{2,1,0:T(8,128)(2,1)S(1)} copy-done((bf16[1,128,4096]{2,1,0:T(8,128)(2,1)S(1)}, bf16[1,128,4096]{2,1,0:T(8,128)(2,1)}, u32[]{:S(2)}) %copy-start) | copy-done | bytes 1048600
  24.4 8.4 %local.1 = (f32[128,4096]{1,0:T(8,128)S(1)}, f32[16,4096]{1,0:T(8,128)S(1)}, f32[8,4096]{1,0:T(8,128)S(1)}) custom-call(f32[16,256]{1,0:T(8,128)S(1)} %copy-done.1, f32[1,4096]{1,0:T(1,128)S(1)} %reshape.30.rate_row_ref, f32[1,4096]{1,0:T(1,128)S(1)} %reshape.31.amp_row_ref, bf16[128,4096]{1,0:T(8,128)(2,1)S(1)} %bitcast.19), custom_call_target="tpu_custom_call" | custom-call | flops 8000000000 | bytes 5242880 | tf_op jit(solution)/shard_map/local/pallas_call | solution.py:311
  32.8 7.8 %all-to-all-done = f32[64,1,2176]{2,1,0:T(1,128)S(1)} async-done(((f32[64,1,2176]{2,1,0:T(1,128)}), f32[64,1,2176]{2,1,0:T(1,128)S(1)}, u32[]{:S(2)}, u32[]{:S(2)}) %all-to-all-start) | async-done | bytes 557088 | tf_op jit(solution)/shard_map/all_to_all | solution.py:300
  40.6 0.3 scan.1
  40.9 19.1 %all_to_all.10 = f32[64,1,1152]{2,1,0:T(1,128)S(1)} all-to-all(f32[64,1,1152]{2,1,0:T(1,128)S(1)} %bitcast.17), channel_id=1, replica_groups=mesh['seq_x'=2,'seq_core'=2,'ctx_0'=2,'ctx_1'=8,'ctx_2'=4] {'ctx_0','ctx..., dimensions={0} | all-to-all | bytes 589824 | tf_op jit(solution)/shard_map/all_to_all | solution.py:344
  60.1 4.2 %collective-permute-start.2 = (f32[32,128]{1,0:T(8,128)S(1)}, f32[32,128]{1,0:T(8,128)S(1)}, u32[]{:S(2)}, u32[]{:S(2)}) collective-permute-start(f32[32,128]{1,0:T(8,128)S(1)} %add_bitcast_fusion.a_ref), channel_id=1, source_target_pairs={{0,192},{64,128},{128,64},{192,0},{1,193},{65,129},{129,65},{193,1... | collective-permute-start | bytes 49160 | tf_op jit(solution)/shard_map/ppermute | solution.py:351
  64.2 1.2 %collective-permute-start.1 = (f32[32,128]{1,0:T(8,128)S(1)}, f32[32,128]{1,0:T(8,128)S(1)}, u32[]{:S(2)}, u32[]{:S(2)}) collective-permute-start(f32[32,128]{1,0:T(8,128)S(1)} %add_bitcast_fusion.a_ref), channel_id=1, source_target_pairs={{0,128},{64,192},{128,0},{192,64},{1,129},{65,193},{129,1},{193,65... | collective-permute-start | bytes 49160 | tf_op jit(solution)/shard_map/ppermute | solution.py:351
  65.4 0.0 collective-permute-start
  65.4 1.8 %carry.1 = f32[128,4096]{1,0:T(8,128)} custom-call(f32[576,128]{1,0:T(8,128)S(1)} %bitcast.16, f32[128,4096]{1,0:T(8,128)S(1)} %get-tuple-element.9.local_ref, f32[16,4096]{1,0:T(8,128)S(1)} %get-tuple-element.10.near_ref, f32[8,4096]{1,0:T(8,128)S(1)} %get-tuple-element.11.far_ref), custom_call_target="tpu_custom_call" | custom-call | flops 800000000 | bytes 7340032 | tf_op jit(solution)/shard_map/carry/pallas_call | solution.py:352
  67.2 0.0 collective-permute-done.2.d_ref
  67.2 0.0 collective-permute-done.1.c_ref
  67.2 0.0 collective-permute-done.b_ref
  67.2 0.8 %finish.1 = f32[16,256]{1,0:T(8,128)} custom-call(f32[16,256]{1,0:T(8,128)S(1)} %get-tuple-element.14.factor_ref, f32[32,128]{1,0:T(8,128)S(1)} %add_bitcast_fusion.a_ref, f32[32,128]{1,0:T(8,128)S(1)} %collective-permute-done.b_ref, f32[32,128]{1,0:T(8,128)S(1)} %collective-permute-done.1.c_ref, f32[32,128]{1,0:T(8,128)S(1)} %collective-permute-done.2.d_ref), custom_call_target="tpu_custom_call" | custom-call | tf_op jit(solution)/shard_map/finish/pallas_call | solution.py:369
  (6 shorter events, 0.1 us)
Async XLA Ops:
  0.6 21.8 %copy-start.1 = (f32[16,256]{1,0:T(8,128)S(1)}, f32[16,256]{1,0:T(8,128)}, u32[]{:S(2)}) copy-start(f32[16,256]{1,0:T(8,128)} %rates_ref.1) | copy-start | bytes 49156
  0.6 22.0 %copy-start.2 = (f32[16,256]{1,0:T(8,128)S(1)}, f32[16,256]{1,0:T(8,128)}, u32[]{:S(2)}) copy-start(f32[16,256]{1,0:T(8,128)} %param.6) | copy-start | bytes 49156
  7.3 33.3 %all-to-all-start = ((f32[64,1,2176]{2,1,0:T(1,128)}), f32[64,1,2176]{2,1,0:T(1,128)S(1)}, u32[]{:S(2)}, u32[]{:S(2)}) async-start(f32[64,1,2176]{2,1,0:T(1,128)} %bitcast.21), calls=%async_computation | async-start | bytes 1114112 | tf_op jit(solution)/shard_map/all_to_all | solution.py:300
  23.1 1.2 %copy-start = (bf16[1,128,4096]{2,1,0:T(8,128)(2,1)S(1)}, bf16[1,128,4096]{2,1,0:T(8,128)(2,1)}, u32[]{:S(2)}) copy-start(bf16[1,128,4096]{2,1,0:T(8,128)(2,1)} %param.4) | copy-start | bytes 3145732
  60.1 7.1 %collective-permute-start.2 = (f32[32,128]{1,0:T(8,128)S(1)}, f32[32,128]{1,0:T(8,128)S(1)}, u32[]{:S(2)}, u32[]{:S(2)}) collective-permute-start(f32[32,128]{1,0:T(8,128)S(1)} %add_bitcast_fusion.a_ref), channel_id=1, source_target_pairs={{0,192},{64,128},{128,64},{192,0},{1,193},{65,129},{129,65},{193,1... | collective-permute-start | bytes 49160 | tf_op jit(solution)/shard_map/ppermute | solution.py:351
  64.2 3.0 %collective-permute-start.1 = (f32[32,128]{1,0:T(8,128)S(1)}, f32[32,128]{1,0:T(8,128)S(1)}, u32[]{:S(2)}, u32[]{:S(2)}) collective-permute-start(f32[32,128]{1,0:T(8,128)S(1)} %add_bitcast_fusion.a_ref), channel_id=1, source_target_pairs={{0,128},{64,192},{128,0},{192,64},{1,129},{65,193},{129,1},{193,65... | collective-permute-start | bytes 49160 | tf_op jit(solution)/shard_map/ppermute | solution.py:351
  65.4 1.8 %collective-permute-start = (f32[32,128]{1,0:T(8,128)S(1)}, f32[32,128]{1,0:T(8,128)S(1)}, u32[]{:S(2)}, u32[]{:S(2)}) collective-permute-start(f32[32,128]{1,0:T(8,128)S(1)} %add_bitcast_fusion.a_ref), channel_id=1, source_target_pairs={{0,64},{64,0},{128,192},{192,128},{1,65},{65,1},{129,193},{193,129... | collective-permute-start | bytes 49160 | tf_op jit(solution)/shard_map/ppermute | solution.py:351
